TPU v7x, 32 devices: a whole 2x2x4 slice. The times are simulated.
32 devices in a mesh: space: 2 (over y), energy: 16 (over z, x, core).
Axes of the slice: x: 2, y: 2, z: 4, core: 2. Of those that a mesh axis runs over, the one named last changes fastest.
Arguments:
- green_lesser: bfloat16 [16, 2, 2, 256, 256], P('energy', 'space'), may hold values from -6 to 6
- screened_lesser: bfloat16 [16, 2, 2, 256, 256], P('energy', 'space'), may hold values from -1.5 to 1.5
- green_retarded: bfloat16 [16, 2, 2, 256, 256], P('energy', 'space'), may hold values from -6 to 6
- screened_retarded: bfloat16 [16, 2, 2, 256, 256], P('energy', 'space'), may hold values from -1.5 to 1.5
- left_green: bfloat16 [16, 2, 2, 256, 256], P('energy', 'space'), may hold values from -0.25 to 0.25
- coupling: bfloat16 [2, 2, 256, 256], P('space'), may hold values from -0.25 to 0.25
Outputs:
- lesser_left: bfloat16 [16, 2, 2, 256, 256], P('energy', 'space')
- sigma_retarded: bfloat16 [16, 2, 2, 256, 256], P('energy', 'space')
All inputs are finite; a program needn't handle non-finite values.
Results may differ from a plain program's by a relative error of at most 0.018.
Values may be sent and summed in bfloat16 or wider, within the bound.
No kernel may reach another device: no remote copies, remote signals or barrier semaphores. Data moves between devices by JAX's collectives and lax.ppermute only.
A program may use at most 64 MiB of HBM per device.

v0:
```python
import math

import jax
import jax.numpy as jnp
from jax import lax
from jax.sharding import PartitionSpec as P


def from_behind(array, axis, by):
    size = lax.axis_size(axis)
    pairs = [(i, i + by) for i in range(size) if 0 <= i + by < size]
    return lax.ppermute(array, axis, pairs)


def contract(einsum_pattern, first_factor, second_factor):
    return jnp.einsum(
        einsum_pattern,
        first_factor,
        second_factor,
        precision=lax.Precision.HIGHEST,
        preferred_element_type=jnp.float32,
    )


def complex_product(einsum_pattern, first_factor, second_factor):
    first_real, first_imag = (first_factor[..., 0, :, :], first_factor[..., 1, :, :])
    second_real, second_imag = (second_factor[..., 0, :, :], second_factor[..., 1, :, :])
    real_part = contract(einsum_pattern, first_real, second_real) - contract(
        einsum_pattern, first_imag, second_imag
    )
    imag_part = contract(einsum_pattern, first_real, second_imag) + contract(
        einsum_pattern, first_imag, second_real
    )
    return jnp.stack([real_part, imag_part], axis=-3)


def adjoint_product(einsum_pattern, first_factor, second_factor):
    first_real, first_imag = (first_factor[..., 0, :, :], first_factor[..., 1, :, :])
    second_real, second_imag = (second_factor[..., 0, :, :], second_factor[..., 1, :, :])
    real_part = contract(einsum_pattern, first_real, second_real) + contract(
        einsum_pattern, first_imag, second_imag
    )
    imag_part = contract(einsum_pattern, first_imag, second_real) - contract(
        einsum_pattern, first_real, second_imag
    )
    return jnp.stack([real_part, imag_part], axis=-3)


def rounded(values):
    return lax.optimization_barrier(values.astype(jnp.bfloat16))


def sandwich(propagator, state):
    inner = complex_product("eij,ejk->eik", propagator, state)
    return adjoint_product("eij,ekj->eik", inner, propagator)


def split_parts(values):
    upper_block = values.astype(jnp.bfloat16)
    lower = (values - upper_block.astype(jnp.float32)).astype(jnp.bfloat16)
    return (upper_block, lower)


def trig_table(phase, length):
    angle = phase.astype(jnp.float32) * (2.0 * math.pi / length)
    return (split_parts(jnp.cos(angle)), split_parts(jnp.sin(angle)))


def table_product(trig_table_pair, slab_values):
    upper_block = jnp.einsum(
        "jz,zgx->jgx", trig_table_pair[0], slab_values, preferred_element_type=jnp.float32
    )
    return upper_block + jnp.einsum(
        "jz,zgx->jgx", trig_table_pair[1], slab_values, preferred_element_type=jnp.float32
    )


def table_product_wide(trig_table_pair, slab_values):
    upper_values, lower_values = split_parts(slab_values)
    total_sum = jnp.einsum(
        "jz,zgx->jgx", trig_table_pair[0], upper_values, preferred_element_type=jnp.float32
    )
    total_sum = total_sum + jnp.einsum(
        "jz,zgx->jgx", trig_table_pair[0], lower_values, preferred_element_type=jnp.float32
    )
    return total_sum + jnp.einsum(
        "jz,zgx->jgx", trig_table_pair[1], upper_values, preferred_element_type=jnp.float32
    )


def transform(table, real_part, imag_part, backward):
    cosine_table, sine_table = table
    if backward:
        cos_real = table_product_wide(cosine_table, real_part)
        cos_imag = table_product_wide(cosine_table, imag_part)
        sin_real = table_product_wide(sine_table, real_part)
        sin_imag = table_product_wide(sine_table, imag_part)
        return (cos_real - sin_imag, cos_imag + sin_real)
    cos_real = table_product(cosine_table, real_part)
    cos_imag = table_product(cosine_table, imag_part)
    sin_real = table_product(sine_table, real_part)
    sin_imag = table_product(sine_table, imag_part)
    return (cos_real + sin_imag, cos_imag - sin_real)


def pair_product(first_pair, second_pair):
    return (
        first_pair[0] * second_pair[0] - first_pair[1] * second_pair[1],
        first_pair[0] * second_pair[1] + first_pair[1] * second_pair[0],
    )


def convolve(pieces):
    piece_shape = pieces[0].shape
    energies_all = piece_shape[0]
    length = 2 * energies_all
    freq_index = jnp.arange(length, dtype=jnp.int32)
    energy_index = jnp.arange(energies_all, dtype=jnp.int32)
    lag_index = energy_index - energies_all // 2
    green_table = trig_table(freq_index[:, None] * energy_index[None, :] % length, length)
    screen_table = trig_table(freq_index[:, None] * lag_index[None, :] % length, length)
    return_table = trig_table(energy_index[:, None] * freq_index[None, :] % length, length)

    def spectrum(stacked, table):
        flat = stacked.reshape(piece_shape[0], piece_shape[1], 2, piece_shape[3] * piece_shape[4])
        return transform(table, flat[:, :, 0], flat[:, :, 1], False)

    green_less = spectrum(pieces[0], green_table)
    screen_less = spectrum(pieces[1], screen_table)
    green_ret = spectrum(pieces[2], green_table)
    screen_ret = spectrum(pieces[3], screen_table)
    lesser_hat = pair_product(green_less, screen_less)
    screen_total = (screen_less[0] + screen_ret[0], screen_less[1] + screen_ret[1])
    first_term = pair_product(green_ret, screen_total)
    second_term = pair_product(green_less, screen_ret)
    retarded_hat = (first_term[0] + second_term[0], first_term[1] + second_term[1])

    def to_energy(spectrum_pair):
        real_part, imag_part = transform(return_table, spectrum_pair[0], spectrum_pair[1], True)
        stacked = jnp.stack([real_part, imag_part], axis=2) * (1.0 / length)
        return stacked.reshape(piece_shape).astype(jnp.bfloat16)

    lesser_sigma = to_energy(lesser_hat)
    retarded_sigma = to_energy(retarded_hat)
    return (
        lax.all_to_all(lesser_sigma, "energy", split_axis=0, concat_axis=3, tiled=True),
        lax.all_to_all(retarded_sigma, "energy", split_axis=0, concat_axis=3, tiled=True),
    )


def body(green_lesser, screened_lesser, green_retarded, screened_retarded, left_green, coupling):
    energy_points, slabs, _, order, _ = green_lesser.shape
    sigma_lesser, sigma_retarded = convolve(
        (
            lax.all_to_all(green_lesser, "energy", split_axis=3, concat_axis=0, tiled=True),
            lax.all_to_all(screened_lesser, "energy", split_axis=3, concat_axis=0, tiled=True),
            lax.all_to_all(green_retarded, "energy", split_axis=3, concat_axis=0, tiled=True),
            lax.all_to_all(screened_retarded, "energy", split_axis=3, concat_axis=0, tiled=True),
        )
    )
    propagator = rounded(complex_product("esij,sjk->esik", left_green, coupling)).astype(
        jnp.float32
    )
    half_source = rounded(complex_product("esij,esjk->esik", left_green, sigma_lesser))
    source = adjoint_product("esij,eskj->esik", half_source, left_green)
    slab_props = jnp.swapaxes(propagator, 0, 1)
    slab_sources = jnp.swapaxes(source, 0, 1)

    def final_state(entering):

        def state_step(state, slab_pair):
            return (slab_pair[1] + sandwich(slab_pair[0], state), None)

        return lax.scan(state_step, entering, (slab_props, slab_sources))[0]

    zero_state = jnp.zeros((energy_points, 2, order, order), jnp.float32)
    position = lax.axis_index("space")
    devices = lax.axis_size("space")

    def relay_turn(turn_index, entering):
        leaving = lax.cond(position == turn_index, final_state, jnp.zeros_like, entering)
        received = from_behind(leaving.astype(jnp.bfloat16), "space", 1).astype(leaving.dtype)
        return jnp.where(position == turn_index + 1, received, entering)

    entering = lax.fori_loop(0, devices - 1, relay_turn, zero_state)

    def slab_step(state, slab_pair):
        new_state = slab_pair[1] + sandwich(slab_pair[0], state)
        return (new_state, new_state.astype(jnp.bfloat16))

    _, outputs = lax.scan(slab_step, entering, (slab_props, slab_sources))
    lesser_left = jnp.swapaxes(outputs, 0, 1)
    return (lesser_left, sigma_retarded)


def solution(mesh):
    in_specs = (
        P("energy", "space", None, None, None),
        P("energy", "space", None, None, None),
        P("energy", "space", None, None, None),
        P("energy", "space", None, None, None),
        P("energy", "space", None, None, None),
        P("space", None, None, None),
    )
    out_specs = (P("energy", "space", None, None, None), P("energy", "space", None, None, None))
    return jax.shard_map(body, mesh=mesh, in_specs=in_specs, out_specs=out_specs, check_vma=False)
```

profile of v0, /device:TPU:0, one launch (start us, length us, event | category | flops | bytes accessed | tf_op | source)
XLA Modules:
  0.0 114.0 jit_solution(2572517882269621919)
XLA Ops:
  0.6 1.9 %copy.20 = bf16[1,1,2,256,256]{4,2,1,0,3:T(2,128)(2,1)} copy(bf16[1,1,2,256,256]{4,3,2,1,0:T(8,128)(2,1)} %param.9) | data formatting | bytes 524288 | tf_op args[1]
  2.6 7.5 %all-to-all-start.1 = ((bf16[1,1,2,256,256]{4,2,1,0,3:T(2,128)(2,1)}), bf16[1,1,2,256,256]{4,2,1,0,3:T(2,128)(2,1)S(1)}, u32[]{:S(2)}, u32[]{:S(2)}) async-start(bf16[1,1,2,256,256]{4,2,1,0,3:T(2,128)(2,1)} %copy.20), calls=%async_computation.1 | async-start | bytes 524288 | tf_op jit(solution)/shard_map/all_to_all | solution.py:156
  10.6 0.7 copy-done.12
  11.3 1.0 copy.28
  12.3 1.0 copy.18
  13.2 1.0 copy.26
  14.8 5.3 %all-to-all-done.1 = bf16[1,1,2,256,256]{4,2,1,0,3:T(2,128)(2,1)S(1)} async-done(((bf16[1,1,2,256,256]{4,2,1,0,3:T(2,128)(2,1)}), bf16[1,1,2,256,256]{4,2,1,0,3:T(2,128)(2,1)S(1)}, u32[]{:S(2)}, u32[]{:S(2)}) %all-to-all-start.1) | async-done | bytes 262176 | tf_op jit(solution)/shard_map/all_to_all | solution.py:156
  20.1 3.5 %all-to-all-start.4 = ((bf16[1,1,2,256,256]{4,2,1,0,3:T(2,128)(2,1)}), bf16[1,1,2,256,256]{4,2,1,0,3:T(2,128)(2,1)S(1)}, u32[]{:S(2)}, u32[]{:S(2)}) async-start(bf16[1,1,2,256,256]{4,2,1,0,3:T(2,128)(2,1)} %copy.28), calls=%async_computation.4 | async-start | bytes 524288 | tf_op jit(solution)/shard_map/all_to_all | solution.py:158
  23.8 1.1 fusion.76
  24.9 1.1 fusion.74
  26.0 1.1 fusion.73
  27.1 6.6 %all-to-all-done.4 = bf16[1,1,2,256,256]{4,2,1,0,3:T(2,128)(2,1)S(1)} async-done(((bf16[1,1,2,256,256]{4,2,1,0,3:T(2,128)(2,1)}), bf16[1,1,2,256,256]{4,2,1,0,3:T(2,128)(2,1)S(1)}, u32[]{:S(2)}, u32[]{:S(2)}) %all-to-all-start.4) | async-done | bytes 262176 | tf_op jit(solution)/shard_map/all_to_all | solution.py:158
  33.6 3.5 %all-to-all-start = ((bf16[1,1,2,256,256]{4,2,1,0,3:T(2,128)(2,1)}), bf16[1,1,2,256,256]{4,2,1,0,3:T(2,128)(2,1)S(1)}, u32[]{:S(2)}, u32[]{:S(2)}) async-start(bf16[1,1,2,256,256]{4,2,1,0,3:T(2,128)(2,1)} %copy.18), calls=%async_computation | async-start | bytes 524288 | tf_op jit(solution)/shard_map/all_to_all | solution.py:155
  37.2 1.1 fusion.75
  38.4 1.1 fusion.86
  39.5 1.1 fusion.84
  40.6 6.6 %all-to-all-done = bf16[1,1,2,256,256]{4,2,1,0,3:T(2,128)(2,1)S(1)} async-done(((bf16[1,1,2,256,256]{4,2,1,0,3:T(2,128)(2,1)}), bf16[1,1,2,256,256]{4,2,1,0,3:T(2,128)(2,1)S(1)}, u32[]{:S(2)}, u32[]{:S(2)}) %all-to-all-start) | async-done | bytes 262176 | tf_op jit(solution)/shard_map/all_to_all | solution.py:155
  47.1 3.7 %all-to-all-start.3 = ((bf16[1,1,2,256,256]{4,2,1,0,3:T(2,128)(2,1)}), bf16[1,1,2,256,256]{4,2,1,0,3:T(2,128)(2,1)S(1)}, u32[]{:S(2)}, u32[]{:S(2)}) async-start(bf16[1,1,2,256,256]{4,2,1,0,3:T(2,128)(2,1)} %copy.26), calls=%async_computation.3 | async-start | bytes 524288 | tf_op jit(solution)/shard_map/all_to_all | solution.py:157
  51.6 1.1 fusion.83
  52.7 1.1 fusion.85
  53.7 6.9 %all-to-all-done.3 = bf16[1,1,2,256,256]{4,2,1,0,3:T(2,128)(2,1)S(1)} async-done(((bf16[1,1,2,256,256]{4,2,1,0,3:T(2,128)(2,1)}), bf16[1,1,2,256,256]{4,2,1,0,3:T(2,128)(2,1)S(1)}, u32[]{:S(2)}, u32[]{:S(2)}) %all-to-all-start.3) | async-done | bytes 262176 | tf_op jit(solution)/shard_map/all_to_all | solution.py:157
  62.5 0.5 copy-done.4
  63.2 0.8 copy-done.5
  64.3 0.8 copy-done.7
  65.0 0.3 convolution_add_fusion.6
  65.3 0.8 copy-done.8
  66.7 0.3 convolution_add_fusion.8
  67.5 0.7 copy-done.1
  68.3 0.3 fusion.15
  68.6 0.8 copy-done.2
  69.3 0.3 fusion.17
  69.6 0.8 copy-done.3
  70.6 0.8 copy-done.6
  71.4 0.3 fusion.21
  71.7 0.3 fusion.14
  72.0 0.3 fusion.18
  72.3 0.3 fusion.20
  72.6 0.7 subtract_add_fusion
  75.4 0.9 convolution_add_fusion.24
  76.6 0.9 convolution_add_fusion.21
  79.5 0.7 fusion.38
  80.2 3.7 %all-to-all-start.2 = ((bf16[16,1,2,16,256]{4,3,2,1,0:T(8,128)(2,1)}), bf16[16,1,2,16,256]{4,3,2,1,0:T(8,128)(2,1)S(1)}, u32[]{:S(2)}, u32[]{:S(2)}) async-start(bf16[16,1,2,16,256]{4,3,2,1,0:T(8,128)(2,1)} %fusion.38), calls=%async_computation.2 | async-start | bytes 524288 | tf_op jit(solution)/shard_map/all_to_all | solution.py:146
  84.1 0.7 copy-done.11
  85.5 0.7 fusion.40
  86.2 7.6 %all-to-all-done.2 = bf16[16,1,2,16,256]{4,3,2,1,0:T(8,128)(2,1)S(1)} async-done(((bf16[16,1,2,16,256]{4,3,2,1,0:T(8,128)(2,1)}), bf16[16,1,2,16,256]{4,3,2,1,0:T(8,128)(2,1)S(1)}, u32[]{:S(2)}, u32[]{:S(2)}) %all-to-all-start.2) | async-done | bytes 262176 | tf_op jit(solution)/shard_map/all_to_all | solution.py:146
  93.9 3.5 %all-to-all-start.5 = ((bf16[16,1,2,16,256]{4,3,2,1,0:T(8,128)(2,1)}), bf16[16,1,2,16,256]{4,3,2,1,0:T(8,128)(2,1)S(1)}, u32[]{:S(2)}, u32[]{:S(2)}) async-start(bf16[16,1,2,16,256]{4,3,2,1,0:T(8,128)(2,1)} %fusion.40), calls=%async_computation.5 | async-start | bytes 524288 | tf_op jit(solution)/shard_map/all_to_all | solution.py:147
  99.5 3.8 %conditional.1 = (bf16[1,2,256,256]{3,2,1,0:T(8,128)(2,1)S(1)}) conditional(s32[]{:T(128)} %convert_element_type.497, () %tuple.20, (f32[1,1,2,256,256]{4,3,2,1,0:T(8,128)S(1)}, f32[1,1,2,256,256]{3,4,2,1,0:T(8,128)S(1)}, f32[1,2,256,256]{3,2,1,0:T(8,128)S(1)}) %tuple.21), branch_computations={%region_0.1_spmd, %region_1.2_spmd} | conditional | flops 1611268096 | bytes 9699336 | solution.py:181
  99.9 0.4 fusion.6
  100.3 0.4 convolution_subtract_fusion.1
  100.7 0.4 fusion.13
  101.1 0.4 fusion.2
  101.5 0.4 convolution_add_fusion.1
  101.9 0.4 fusion.1
  102.3 0.4 fusion.12
  102.7 0.4 fusion
  103.2 1.3 %collective-permute-start = (bf16[1,2,256,256]{3,2,1,0:T(8,128)(2,1)S(1)}, bf16[1,2,256,256]{3,2,1,0:T(8,128)(2,1)S(1)}, u32[]{:S(2)}, u32[]{:S(2)}) collective-permute-start(bf16[1,2,256,256]{3,2,1,0:T(8,128)(2,1)S(1)} %get-tuple-element.73), channel_id=1, source_target_pairs={{0,16},{1,17},{2,18},{3,19},{4,20},{5,21},{6,22},{7,23},{8,24},{9,... | collective-permute-start | bytes 786440 | tf_op jit(solution)/shard_map/while/body/eval_jaxpr/ppermute | solution.py:12
  104.5 2.9 %all-to-all-done.5 = bf16[16,1,2,16,256]{4,3,2,1,0:T(8,128)(2,1)S(1)} async-done(((bf16[16,1,2,16,256]{4,3,2,1,0:T(8,128)(2,1)}), bf16[16,1,2,16,256]{4,3,2,1,0:T(8,128)(2,1)S(1)}, u32[]{:S(2)}, u32[]{:S(2)}) %all-to-all-start.5) | async-done | bytes 262176 | tf_op jit(solution)/shard_map/all_to_all | solution.py:147
  107.4 0.7 copy.32
  108.1 2.7 %collective-permute-done = bf16[1,2,256,256]{3,2,1,0:T(8,128)(2,1)S(1)} collective-permute-done((bf16[1,2,256,256]{3,2,1,0:T(8,128)(2,1)S(1)}, bf16[1,2,256,256]{3,2,1,0:T(8,128)(2,1)S(1)}, u32[]{:S(2)}, u32[]{:S(2)}) %collective-permute-start) | collective-permute-done | bytes 262176 | tf_op jit(solution)/shard_map/while/body/eval_jaxpr/ppermute | solution.py:12
  110.8 0.3 fusion.42
  111.2 0.3 fusion.41
  111.5 0.3 convolution_subtract_fusion.3
  112.1 0.3 convolution_add_fusion.35
  113.3 0.8 fusion.39
  (95 shorter events, 14.1 us)
Async XLA Ops:
  2.6 7.5 %copy-start = (bf16[1,1,2,256,256]{4,3,2,1,0:T(8,128)(2,1)S(1)}, bf16[1,1,2,256,256]{4,3,2,1,0:T(8,128)(2,1)}, u32[]{:S(2)}) copy-start(bf16[1,1,2,256,256]{4,3,2,1,0:T(8,128)(2,1)} %param.12) | copy-start | bytes 786436
  2.6 7.5 %copy-start.9 = (bf16[1,2,256,256]{3,2,1,0:T(8,128)(2,1)S(1)}, bf16[1,2,256,256]{3,2,1,0:T(8,128)(2,1)}, u32[]{:S(2)}) copy-start(bf16[1,2,256,256]{3,2,1,0:T(8,128)(2,1)} %param.13) | copy-start | bytes 786436
  2.6 17.5 %all-to-all-start.1 = ((bf16[1,1,2,256,256]{4,2,1,0,3:T(2,128)(2,1)}), bf16[1,1,2,256,256]{4,2,1,0,3:T(2,128)(2,1)S(1)}, u32[]{:S(2)}, u32[]{:S(2)}) async-start(bf16[1,1,2,256,256]{4,2,1,0,3:T(2,128)(2,1)} %copy.20), calls=%async_computation.1 | async-start | bytes 524288 | tf_op jit(solution)/shard_map/all_to_all | solution.py:156
  10.3 1.0 copy-start.12
  11.3 1.0 copy-start.13
  12.3 1.0 copy-start.14
  20.1 13.5 %all-to-all-start.4 = ((bf16[1,1,2,256,256]{4,2,1,0,3:T(2,128)(2,1)}), bf16[1,1,2,256,256]{4,2,1,0,3:T(2,128)(2,1)S(1)}, u32[]{:S(2)}, u32[]{:S(2)}) async-start(bf16[1,1,2,256,256]{4,2,1,0,3:T(2,128)(2,1)} %copy.28), calls=%async_computation.4 | async-start | bytes 524288 | tf_op jit(solution)/shard_map/all_to_all | solution.py:158
  33.6 13.5 %all-to-all-start = ((bf16[1,1,2,256,256]{4,2,1,0,3:T(2,128)(2,1)}), bf16[1,1,2,256,256]{4,2,1,0,3:T(2,128)(2,1)S(1)}, u32[]{:S(2)}, u32[]{:S(2)}) async-start(bf16[1,1,2,256,256]{4,2,1,0,3:T(2,128)(2,1)} %copy.18), calls=%async_computation | async-start | bytes 524288 | tf_op jit(solution)/shard_map/all_to_all | solution.py:155
  47.1 13.5 %all-to-all-start.3 = ((bf16[1,1,2,256,256]{4,2,1,0,3:T(2,128)(2,1)}), bf16[1,1,2,256,256]{4,2,1,0,3:T(2,128)(2,1)S(1)}, u32[]{:S(2)}, u32[]{:S(2)}) async-start(bf16[1,1,2,256,256]{4,2,1,0,3:T(2,128)(2,1)} %copy.26), calls=%async_computation.3 | async-start | bytes 524288 | tf_op jit(solution)/shard_map/all_to_all | solution.py:157
  61.9 1.0 copy-start.4
  63.0 1.0 copy-start.5
  64.0 1.0 copy-start.7
  65.0 1.0 copy-start.8
  67.2 1.0 copy-start.1
  68.3 1.0 copy-start.2
  69.3 1.0 copy-start.3
  70.4 1.0 copy-start.6
  80.2 3.7 %copy-start.10 = (f32[16,4096]{1,0:T(8,128)S(1)}, f32[16,4096]{1,0:T(8,128)}, u32[]{:S(2)}) copy-start(f32[16,4096]{1,0:T(8,128)} %convolution_add_fusion.24) | copy-start | bytes 786436
  80.2 13.7 %all-to-all-start.2 = ((bf16[16,1,2,16,256]{4,3,2,1,0:T(8,128)(2,1)}), bf16[16,1,2,16,256]{4,3,2,1,0:T(8,128)(2,1)S(1)}, u32[]{:S(2)}, u32[]{:S(2)}) async-start(bf16[16,1,2,16,256]{4,3,2,1,0:T(8,128)(2,1)} %fusion.38), calls=%async_computation.2 | async-start | bytes 524288 | tf_op jit(solution)/shard_map/all_to_all | solution.py:146
  83.9 1.0 copy-start.11
  93.9 13.5 %all-to-all-start.5 = ((bf16[16,1,2,16,256]{4,3,2,1,0:T(8,128)(2,1)}), bf16[16,1,2,16,256]{4,3,2,1,0:T(8,128)(2,1)S(1)}, u32[]{:S(2)}, u32[]{:S(2)}) async-start(bf16[16,1,2,16,256]{4,3,2,1,0:T(8,128)(2,1)} %fusion.40), calls=%async_computation.5 | async-start | bytes 524288 | tf_op jit(solution)/shard_map/all_to_all | solution.py:147
  103.2 7.6 %collective-permute-start = (bf16[1,2,256,256]{3,2,1,0:T(8,128)(2,1)S(1)}, bf16[1,2,256,256]{3,2,1,0:T(8,128)(2,1)S(1)}, u32[]{:S(2)}, u32[]{:S(2)}) collective-permute-start(bf16[1,2,256,256]{3,2,1,0:T(8,128)(2,1)S(1)} %get-tuple-element.73), channel_id=1, source_target_pairs={{0,16},{1,17},{2,18},{3,19},{4,20},{5,21},{6,22},{7,23},{8,24},{9,... | collective-permute-start | bytes 786440 | tf_op jit(solution)/shard_map/while/body/eval_jaxpr/ppermute | solution.py:12
where the time goes:
time: 115 us; the launch traced here: 114 us
  waiting for transfers between devices  38.6 us (34%)
  matrix products  30.5 us (27%)
  starting transfers between devices  26.8 us (23%)
  local copies, waits for them, and re-layouts  14 us (12%)
  other arithmetic  2.51 us (2%)
  between operations  1.4 us (1%)
    unnamed x38, local copies, waits for them, and re-layouts  12.4 us
    dot_general x16, matrix products, table_product(): jnp.einsum('jz,zgx->jgx', trig_table_pair[0], slab_values, preferred_elem...  10.8 us
    dot_general x28, matrix products, contract(): jnp.einsum(einsum_pattern, first_factor, second_factor, precision=lax.Pre...  8.26 us
    all_to_all x1, waiting for transfers between devices, convolve(): lax.all_to_all(lesser_sigma, 'energy', split_axis=0, concat_axis=3, tiled...  7.64 us
    all_to_all x1, starting transfers between devices, body(): lax.all_to_all(screened_lesser, 'energy', split_axis=3, concat_axis=0, ti...  7.52 us
    all_to_all x1, waiting for transfers between devices, body(): lax.all_to_all(green_retarded, 'energy', split_axis=3, concat_axis=0, til...  6.94 us
    all_to_all x1, waiting for transfers between devices, body(): lax.all_to_all(screened_retarded, 'energy', split_axis=3, concat_axis=0,...  6.56 us
    all_to_all x1, waiting for transfers between devices, body(): lax.all_to_all(green_lesser, 'energy', split_axis=3, concat_axis=0, tiled...  6.56 us
  transfers between devices with their start and end apart: 7, of which 7 were waited for; matrix products, arithmetic and copies ran while one was open for 19% of the time, Pallas kernels for 0%

commit v1 on v0

v1 whole, which is shorter than its diff:
```python
import functools

import jax
import jax.numpy as jnp
from jax import lax
from jax.experimental import pallas as pl
from jax.experimental.pallas import tpu as pltpu
from jax.sharding import PartitionSpec as P

VMEM = pl.BlockSpec(memory_space=pltpu.VMEM)
F32, BF16 = jnp.float32, jnp.bfloat16


def call(kernel, outs, args, flops, name):
    moved = sum(a.size * a.dtype.itemsize for a in args)
    moved += sum(o.size * o.dtype.itemsize for o in outs)
    return pl.pallas_call(
        kernel,
        out_shape=outs,
        in_specs=[VMEM] * len(args),
        out_specs=[VMEM] * len(outs),
        cost_estimate=pl.CostEstimate(flops=flops, bytes_accessed=moved, transcendentals=0),
        name=name,
    )(*args)


def shaped(shape, dtype):
    return jax.ShapeDtypeStruct(shape, dtype)


def pack_kernel(first, second, out):
    parts, _, _, rows, columns = out.shape
    for position, source in enumerate((first, second)):
        for entry in range(2):
            out[:, position, entry] = source[entry].reshape(parts, rows, columns)


def pack(first, second, parts):
    _, order, columns = first.shape
    out = shaped((parts, 2, 2, order // parts, columns), first.dtype)
    return call(pack_kernel, [out], [first, second], 0, "pack")[0]


def real_convolution(first, second, energies):
    middle = energies // 2
    sums = []
    for n in range(energies):
        total = None
        for m in range(energies):
            lag = n - m + middle
            if 0 <= lag < energies:
                term = first[m] * second[lag]
                total = term if total is None else total + term
        sums.append(total)
    return sums


def complex_convolution(load_first, load_second, store, energies):
    if energies <= 16:
        span = range(energies)
        both = real_convolution(
            [load_first(m, 0) + load_first(m, 1) for m in span],
            [load_second(j, 0) for j in span],
            energies,
        )
        cross = real_convolution(
            [load_first(m, 0) for m in span],
            [load_second(j, 1) - load_second(j, 0) for j in span],
            energies,
        )
        other = real_convolution(
            [load_first(m, 1) for m in span],
            [load_second(j, 0) + load_second(j, 1) for j in span],
            energies,
        )
        for n in span:
            store(n, both[n] - other[n], both[n] + cross[n])
        return
    middle = energies // 2

    def one_energy(n, carry):
        def one_term(m, sums):
            lag = n - m + middle
            a, b = load_first(m, 0), load_first(m, 1)
            c, d = load_second(lag, 0), load_second(lag, 1)
            return (sums[0] + (a * c - b * d), sums[1] + (a * d + b * c))

        zero = jnp.zeros(load_first(0, 0).shape, F32)
        low = jnp.maximum(n + middle - energies + 1, 0)
        high = jnp.minimum(n + middle, energies - 1) + 1
        real, imag = lax.fori_loop(low, high, one_term, (zero, zero))
        store(n, real, imag)
        return carry

    lax.fori_loop(0, energies, one_energy, 0)


def tiles(rows, columns):
    high = 8 if rows % 8 == 0 else rows
    wide = 128 if columns % 128 == 0 else columns
    return high, wide, columns // wide, (rows // high) * (columns // wide)


def each_tile(rows, columns, work):
    high, wide, across, count = tiles(rows, columns)

    def step(i, carry):
        row = pl.multiple_of((i // across) * high, high)
        column = pl.multiple_of((i % across) * wide, wide)
        work(pl.ds(row, high), pl.ds(column, wide))
        return carry

    lax.fori_loop(0, count, step, 0)


def lesser_kernel(data, out, exact):
    energies, _, rows, columns = out.shape

    def work(r, c):
        def store(n, real, imag):
            for entry, value in enumerate((real, imag)):
                exact[n, entry, r, c] = value
                out[n, entry, r, c] = value.astype(out.dtype)

        complex_convolution(
            lambda m, entry: data[m, 0, entry, r, c].astype(F32),
            lambda j, entry: data[j, 1, entry, r, c].astype(F32),
            store,
            energies,
        )

    each_tile(rows, columns, work)


def retarded_kernel(lesser, retarded, exact, out):
    energies, _, rows, columns = out.shape

    def work(r, c):
        def both(index, which, entry):
            left = lesser[index, which, entry, r, c].astype(F32)
            return left + retarded[index, which, entry, r, c].astype(F32)

        def store(n, real, imag):
            for entry, value in enumerate((real, imag)):
                out[n, entry, r, c] = (value - exact[n, entry, r, c]).astype(out.dtype)

        complex_convolution(
            lambda m, entry: both(m, 0, entry),
            lambda j, entry: both(j, 1, entry),
            store,
            energies,
        )

    each_tile(rows, columns, work)


def lesser_convolution(data):
    energies, _, _, rows, columns = data.shape
    shape = (energies, 2, rows, columns)
    flops = 9 * energies * energies * rows * columns
    return call(lesser_kernel, [shaped(shape, BF16), shaped(shape, F32)], [data], flops, "lesser")


def retarded_convolution(lesser, retarded, exact):
    energies, _, _, rows, columns = lesser.shape
    flops = 9 * energies * energies * rows * columns
    out = shaped((energies, 2, rows, columns), BF16)
    return call(retarded_kernel, [out], [lesser, retarded, exact], flops, "retarded")[0]


def dot(first, second):
    return lax.dot_general(first, second, (((1,), (0,)), ((), ())), preferred_element_type=F32)


def dot_t(first, second):
    return lax.dot_general(first, second, (((1,), (1,)), ((), ())), preferred_element_type=F32)


def product(a, b, c, d):
    return dot(a, c) - dot(b, d), dot(a, d) + dot(b, c)


def adjoint(a, b, c, d):
    return dot_t(a, c) + dot_t(b, d), dot_t(b, c) - dot_t(a, d)


def propagator_kernel(left, coupling, out):
    real, imag = product(left[0], left[1], coupling[0], coupling[1])
    out[0] = real.astype(out.dtype)
    out[1] = imag.astype(out.dtype)


def source_kernel(left, sigma, out, sent):
    order = left.shape[1]
    s_real = sigma[:, 0].reshape(order, order)
    s_imag = sigma[:, 1].reshape(order, order)
    real, imag = product(left[0], left[1], s_real, s_imag)
    real, imag = adjoint(real.astype(BF16), imag.astype(BF16), left[0], left[1])
    out[0] = real
    out[1] = imag
    sent[0] = real.astype(sent.dtype)
    sent[1] = imag.astype(sent.dtype)


def split(values):
    upper = values.astype(BF16)
    return upper, (values - upper.astype(F32)).astype(BF16)


def state_kernel(source, propagator, entering, out):
    p_real, p_imag = propagator[0], propagator[1]
    real, imag = product(p_real, p_imag, entering[0], entering[1])
    (real, real_low), (imag, imag_low) = split(real), split(imag)
    new_real, new_imag = adjoint(real, imag, p_real, p_imag)
    low_real, low_imag = adjoint(real_low, imag_low, p_real, p_imag)
    out[0] = (source[0] + (new_real + low_real)).astype(out.dtype)
    out[1] = (source[1] + (new_imag + low_imag)).astype(out.dtype)


def unpack_kernel(sigma, out):
    order = out.shape[1]
    for entry in range(2):
        out[entry] = sigma[:, entry].reshape(order, order)


def body(green_lesser, screened_lesser, green_retarded, screened_retarded, left_green, coupling):
    block = green_lesser.shape[2:]
    order = block[-1]
    assert green_lesser.shape[:2] == (1, 1) and coupling.shape[0] == 1
    parts = lax.axis_size("energy")
    exchange = functools.partial(
        lax.all_to_all, axis_name="energy", split_axis=0, concat_axis=0, tiled=True
    )
    green_l, screen_l = green_lesser.reshape(block), screened_lesser.reshape(block)
    green_r, screen_r = green_retarded.reshape(block), screened_retarded.reshape(block)
    left, hop = left_green.reshape(block), coupling.reshape(block)
    cube = 8 * order**3

    lesser = exchange(pack(green_l, screen_l, parts))
    retarded = exchange(pack(green_r, screen_r, parts))
    sigma_lesser, exact = lesser_convolution(lesser)
    sigma_lesser = exchange(sigma_lesser)
    sigma_retarded = exchange(retarded_convolution(lesser, retarded, exact))

    propagator = call(propagator_kernel, [shaped(block, BF16)], [left, hop], cube, "propagator")[0]
    source, state = call(
        source_kernel,
        [shaped(block, F32), shaped(block, BF16)],
        [left, sigma_lesser],
        2 * cube,
        "source",
    )
    devices = lax.axis_size("space")
    pairs = [(i, i + 1) for i in range(devices - 1)]
    for _ in range(devices - 1):
        entering = lax.ppermute(state, "space", pairs)
        state = call(
            state_kernel, [shaped(block, BF16)], [source, propagator, entering], 3 * cube, "state"
        )[0]
    retarded_out = call(unpack_kernel, [shaped(block, BF16)], [sigma_retarded], 0, "unpack")[0]
    return state.reshape(left_green.shape), retarded_out.reshape(left_green.shape)


def solution(mesh):
    split_spec = P("energy", "space", None, None, None)
    return jax.shard_map(
        body,
        mesh=mesh,
        in_specs=(split_spec,) * 5 + (P("space", None, None, None),),
        out_specs=(split_spec, split_spec),
        check_vma=False,
    )
```

time: 115 us -> 77.5 us (0.67)
  matrix products: 30.5 us -> 0 us
  Pallas kernels: 0 us -> 18.3 us
  local copies, waits for them, and re-layouts: 14 us -> 2.15 us
  waiting for transfers between devices: 38.6 us -> 33 us
  starting transfers between devices: 26.8 us -> 22.7 us
  other arithmetic: 2.51 us -> 0 us
    dot_general x84 -> x0, matrix products: 30.5 us -> none  [the longest x16 10.8 us: table_product(): jnp.einsum('jz,zgx->jgx', trig_table_pair[0], slab_values, preferred_elem...]
    pallas_call x0 -> x8, Pallas kernels: none -> 18.3 us  [call(): pl.pallas_call(kernel, out_shape=outs, in_specs=[VMEM] * len(args), out_s...]
    unnamed x38 -> x10, local copies, waits for them, and re-layouts: 12.4 us -> 2.15 us
    all_to_all x6 -> x4, starting transfers between devices: 25.5 us -> 19.2 us  [the longest x1 7.39 us: body(): lesser = exchange(pack(green_l, screen_l, parts))]
    all_to_all x6 -> x4, waiting for transfers between devices: 35.9 us -> 33 us  [the longest x1 12.4 us: body(): lesser = exchange(pack(green_l, screen_l, parts))]
    ppermute x1, waiting for transfers between devices: 2.68 us -> 0.01 us  [body(): entering = lax.ppermute(state, 'space', pairs)]
    convert_element_type x4 -> x0, other arithmetic: 2.3 us -> none  [the longest x2 1.5 us: to_energy(): return stacked.reshape(piece_shape).astype(jnp.bfloat16)]
    ppermute x1, starting transfers between devices: 1.31 us -> 3.43 us  [body(): entering = lax.ppermute(state, 'space', pairs)]
  transfers between devices with their start and end apart: 7 -> 5, of which waited for: 7 -> 4; matrix products, arithmetic and copies ran while one was open for 19% -> 0% of each run, Pallas kernels for 0% -> 18%
where the time goes in v1:
time: 77.5 us; the launch traced here: 76.8 us
  waiting for transfers between devices  33 us (43%)
  starting transfers between devices  22.7 us (29%)
  Pallas kernels  18.3 us (24%)
  local copies, waits for them, and re-layouts  2.15 us (3%)
    pallas_call x8, Pallas kernels, call(): pl.pallas_call(kernel, out_shape=outs, in_specs=[VMEM] * len(args), out_s...  18.3 us
    all_to_all x1, waiting for transfers between devices, body(): lesser = exchange(pack(green_l, screen_l, parts))  12.4 us
    all_to_all x1, waiting for transfers between devices, body(): retarded = exchange(pack(green_r, screen_r, parts))  11.6 us
    all_to_all x1, starting transfers between devices, body(): lesser = exchange(pack(green_l, screen_l, parts))  7.39 us
    all_to_all x1, waiting for transfers between devices, body(): sigma_lesser = exchange(sigma_lesser)  7.06 us
    all_to_all x1, starting transfers between devices, body(): sigma_lesser = exchange(sigma_lesser)  4.16 us
    all_to_all x1, starting transfers between devices, body(): retarded = exchange(pack(green_r, screen_r, parts))  4.16 us
    all_to_all x1, starting transfers between devices, body(): sigma_retarded = exchange(retarded_convolution(lesser, retarded, exact))  3.53 us
  transfers between devices with their start and end apart: 5, of which 4 were waited for; matrix products, arithmetic and copies ran while one was open for 0% of the time, Pallas kernels for 18%

profile of v1, /device:TPU:0, one launch (start us, length us, event | category | flops | bytes accessed | tf_op | source)
XLA Modules:
  0.0 76.8 jit_solution(11333487254802696176)
XLA Ops:
  0.6 1.9 %pack.2 = bf16[16,2,2,16,256]{4,3,2,1,0:T(8,128)(2,1)} custom-call(bf16[2,256,256]{2,1,0:T(8,128)(2,1)} %bitcast.12, bf16[2,256,256]{2,1,0:T(8,128)(2,1)} %bitcast.13), custom_call_target="tpu_custom_call" | custom-call | bytes 1048576 | tf_op jit(solution)/shard_map/pack/pallas_call | solution.py:17
  2.5 7.4 %all-to-all-start = ((bf16[16,2,2,16,256]{4,3,2,1,0:T(8,128)(2,1)}), bf16[16,2,2,16,256]{4,3,2,1,0:T(8,128)(2,1)S(1)}, u32[]{:S(2)}, u32[]{:S(2)}) async-start(bf16[16,2,2,16,256]{4,3,2,1,0:T(8,128)(2,1)} %pack.2), calls=%async_computation | async-start | bytes 1048576 | tf_op jit(solution)/shard_map/all_to_all | solution.py:239
  9.9 1.9 %pack.3 = bf16[16,2,2,16,256]{4,3,2,1,0:T(8,128)(2,1)} custom-call(bf16[2,256,256]{2,1,0:T(8,128)(2,1)} %bitcast.14, bf16[2,256,256]{2,1,0:T(8,128)(2,1)} %bitcast.15), custom_call_target="tpu_custom_call" | custom-call | bytes 1048576 | tf_op jit(solution)/shard_map/pack/pallas_call | solution.py:17
  11.8 12.4 %all-to-all-done.data.lesser = bf16[16,2,2,16,256]{4,3,2,1,0:T(8,128)(2,1)S(1)} async-done(((bf16[16,2,2,16,256]{4,3,2,1,0:T(8,128)(2,1)}), bf16[16,2,2,16,256]{4,3,2,1,0:T(8,128)(2,1)S(1)}, u32[]{:S(2)}, u32[]{:S(2)}) %all-to-all-start) | async-done | bytes 524320 | tf_op jit(solution)/shard_map/all_to_all | solution.py:239
  24.1 0.0 copy-start
  24.1 4.2 %all-to-all-start.2 = ((bf16[16,2,2,16,256]{4,3,2,1,0:T(8,128)(2,1)}), bf16[16,2,2,16,256]{4,3,2,1,0:T(8,128)(2,1)S(1)}, u32[]{:S(2)}, u32[]{:S(2)}) async-start(bf16[16,2,2,16,256]{4,3,2,1,0:T(8,128)(2,1)} %pack.3), calls=%async_computation.2 | async-start | bytes 1048576 | tf_op jit(solution)/shard_map/all_to_all | solution.py:240
  28.3 0.0 copy-done
  28.3 2.7 %lesser.1 = (bf16[16,2,16,256]{3,2,1,0:T(8,128)(2,1)}, f32[16,2,16,256]{3,2,1,0:T(8,128)}) custom-call(bf16[16,2,2,16,256]{4,3,2,1,0:T(8,128)(2,1)} %copy-done), custom_call_target="tpu_custom_call" | custom-call | flops 9437184 | bytes 1310720 | tf_op jit(solution)/shard_map/lesser/pallas_call | solution.py:17
  31.0 11.6 %all-to-all-done.2.retarded = bf16[16,2,2,16,256]{4,3,2,1,0:T(8,128)(2,1)S(1)} async-done(((bf16[16,2,2,16,256]{4,3,2,1,0:T(8,128)(2,1)}), bf16[16,2,2,16,256]{4,3,2,1,0:T(8,128)(2,1)S(1)}, u32[]{:S(2)}, u32[]{:S(2)}) %all-to-all-start.2) | async-done | bytes 524320 | tf_op jit(solution)/shard_map/all_to_all | solution.py:240
  42.6 0.0 copy-start.1
  42.6 4.2 %all-to-all-start.1 = ((bf16[16,2,16,256]{3,2,1,0:T(8,128)(2,1)}), bf16[16,2,16,256]{3,2,1,0:T(8,128)(2,1)S(1)}, u32[]{:S(2)}, u32[]{:S(2)}) async-start(bf16[16,2,16,256]{3,2,1,0:T(8,128)(2,1)} %get-tuple-element.6), calls=%async_computation.1 | async-start | bytes 524288 | tf_op jit(solution)/shard_map/all_to_all | solution.py:242
  46.8 0.0 copy-done.1
  46.8 2.9 %retarded.1 = bf16[16,2,16,256]{3,2,1,0:T(8,128)(2,1)} custom-call(bf16[16,2,2,16,256]{4,3,2,1,0:T(8,128)(2,1)} %copy-done, bf16[16,2,2,16,256]{4,3,2,1,0:T(8,128)(2,1)} %copy-done.1, f32[16,2,16,256]{3,2,1,0:T(8,128)} %get-tuple-element.9.exact), custom_call_target="tpu_custom_call" | custom-call | flops 9437184 | bytes 1835008 | tf_op jit(solution)/shard_map/retarded/pallas_call | solution.py:17
  49.7 7.1 %all-to-all-done.1.sigma = bf16[16,2,16,256]{3,2,1,0:T(8,128)(2,1)S(1)} async-done(((bf16[16,2,16,256]{3,2,1,0:T(8,128)(2,1)}), bf16[16,2,16,256]{3,2,1,0:T(8,128)(2,1)S(1)}, u32[]{:S(2)}, u32[]{:S(2)}) %all-to-all-start.1) | async-done | bytes 262176 | tf_op jit(solution)/shard_map/all_to_all | solution.py:242
  56.8 0.0 copy-start.3
  56.8 0.7 copy-done.3
  57.5 3.5 %all-to-all-start.3 = ((bf16[16,2,16,256]{3,2,1,0:T(8,128)(2,1)}), bf16[16,2,16,256]{3,2,1,0:T(8,128)(2,1)S(1)}, u32[]{:S(2)}, u32[]{:S(2)}) async-start(bf16[16,2,16,256]{3,2,1,0:T(8,128)(2,1)} %retarded.1), calls=%async_computation.3 | async-start | bytes 524288 | tf_op jit(solution)/shard_map/all_to_all | solution.py:243
  61.0 2.6 %source.1 = (f32[2,256,256]{2,1,0:T(8,128)}, bf16[2,256,256]{2,1,0:T(8,128)(2,1)}) custom-call(bf16[2,256,256]{2,1,0:T(8,128)(2,1)} %bitcast.8, bf16[16,2,16,256]{3,2,1,0:T(8,128)(2,1)} %copy-done.3), custom_call_target="tpu_custom_call" | custom-call | flops 268435456 | bytes 1310720 | tf_op jit(solution)/shard_map/source/pallas_call | solution.py:17
  63.6 3.4 %collective-permute-start = (bf16[2,256,256]{2,1,0:T(8,128)(2,1)}, bf16[2,256,256]{2,1,0:T(8,128)(2,1)S(1)}, u32[]{:S(2)}, u32[]{:S(2)}) collective-permute-start(bf16[2,256,256]{2,1,0:T(8,128)(2,1)} %get-tuple-element.8), channel_id=1, source_target_pairs={{0,16},{1,17},{2,18},{3,19},{4,20},{5,21},{6,22},{7,23},{8,24},{9,... | collective-permute-start | bytes 786440 | tf_op jit(solution)/shard_map/ppermute | solution.py:256
  67.0 2.0 %propagator.1 = bf16[2,256,256]{2,1,0:T(8,128)(2,1)} custom-call(bf16[2,256,256]{2,1,0:T(8,128)(2,1)} %bitcast.9, bf16[2,256,256]{2,1,0:T(8,128)(2,1)} %bitcast.10), custom_call_target="tpu_custom_call" | custom-call | flops 134217728 | bytes 786432 | tf_op jit(solution)/shard_map/propagator/pallas_call | solution.py:17
  69.1 1.9 %all-to-all-done.3.sigma = bf16[16,2,16,256]{3,2,1,0:T(8,128)(2,1)S(1)} async-done(((bf16[16,2,16,256]{3,2,1,0:T(8,128)(2,1)}), bf16[16,2,16,256]{3,2,1,0:T(8,128)(2,1)S(1)}, u32[]{:S(2)}, u32[]{:S(2)}) %all-to-all-start.3) | async-done | bytes 262176 | tf_op jit(solution)/shard_map/all_to_all | solution.py:243
  71.0 0.0 copy-start.2
  71.0 0.7 copy-done.2
  71.7 1.7 %unpack.1 = bf16[2,256,256]{2,1,0:T(8,128)(2,1)} custom-call(bf16[16,2,16,256]{3,2,1,0:T(8,128)(2,1)} %copy-done.2), custom_call_target="tpu_custom_call" | custom-call | bytes 524288 | tf_op jit(solution)/shard_map/unpack/pallas_call | solution.py:17
  73.4 0.0 collective-permute-done.entering
  73.4 0.0 copy-start.4
  73.4 0.7 copy-done.4
  74.1 2.7 %state.1 = bf16[2,256,256]{2,1,0:T(8,128)(2,1)} custom-call(f32[2,256,256]{2,1,0:T(8,128)} %get-tuple-element.7.source, bf16[2,256,256]{2,1,0:T(8,128)(2,1)} %propagator.1, bf16[2,256,256]{2,1,0:T(8,128)(2,1)} %copy-done.4), custom_call_target="tpu_custom_call" | custom-call | flops 402653184 | bytes 1310720 | tf_op jit(solution)/shard_map/state/pallas_call | solution.py:17
Async XLA Ops:
  2.5 21.7 %all-to-all-start = ((bf16[16,2,2,16,256]{4,3,2,1,0:T(8,128)(2,1)}), bf16[16,2,2,16,256]{4,3,2,1,0:T(8,128)(2,1)S(1)}, u32[]{:S(2)}, u32[]{:S(2)}) async-start(bf16[16,2,2,16,256]{4,3,2,1,0:T(8,128)(2,1)} %pack.2), calls=%async_computation | async-start | bytes 1048576 | tf_op jit(solution)/shard_map/all_to_all | solution.py:239
  24.1 4.2 %copy-start = (bf16[16,2,2,16,256]{4,3,2,1,0:T(8,128)(2,1)}, bf16[16,2,2,16,256]{4,3,2,1,0:T(8,128)(2,1)S(1)}, u32[]{:S(2)}) copy-start(bf16[16,2,2,16,256]{4,3,2,1,0:T(8,128)(2,1)S(1)} %all-to-all-done.data.lesser) | copy-start | bytes 1572868
  24.1 18.4 %all-to-all-start.2 = ((bf16[16,2,2,16,256]{4,3,2,1,0:T(8,128)(2,1)}), bf16[16,2,2,16,256]{4,3,2,1,0:T(8,128)(2,1)S(1)}, u32[]{:S(2)}, u32[]{:S(2)}) async-start(bf16[16,2,2,16,256]{4,3,2,1,0:T(8,128)(2,1)} %pack.3), calls=%async_computation.2 | async-start | bytes 1048576 | tf_op jit(solution)/shard_map/all_to_all | solution.py:240
  42.6 4.2 %copy-start.1 = (bf16[16,2,2,16,256]{4,3,2,1,0:T(8,128)(2,1)}, bf16[16,2,2,16,256]{4,3,2,1,0:T(8,128)(2,1)S(1)}, u32[]{:S(2)}) copy-start(bf16[16,2,2,16,256]{4,3,2,1,0:T(8,128)(2,1)S(1)} %all-to-all-done.2.retarded) | copy-start | bytes 1572868
  42.6 14.2 %all-to-all-start.1 = ((bf16[16,2,16,256]{3,2,1,0:T(8,128)(2,1)}), bf16[16,2,16,256]{3,2,1,0:T(8,128)(2,1)S(1)}, u32[]{:S(2)}, u32[]{:S(2)}) async-start(bf16[16,2,16,256]{3,2,1,0:T(8,128)(2,1)} %get-tuple-element.6), calls=%async_computation.1 | async-start | bytes 524288 | tf_op jit(solution)/shard_map/all_to_all | solution.py:242
  56.8 0.7 copy-start.3
  57.5 13.5 %all-to-all-start.3 = ((bf16[16,2,16,256]{3,2,1,0:T(8,128)(2,1)}), bf16[16,2,16,256]{3,2,1,0:T(8,128)(2,1)S(1)}, u32[]{:S(2)}, u32[]{:S(2)}) async-start(bf16[16,2,16,256]{3,2,1,0:T(8,128)(2,1)} %retarded.1), calls=%async_computation.3 | async-start | bytes 524288 | tf_op jit(solution)/shard_map/all_to_all | solution.py:243
  63.6 9.8 %collective-permute-start = (bf16[2,256,256]{2,1,0:T(8,128)(2,1)}, bf16[2,256,256]{2,1,0:T(8,128)(2,1)S(1)}, u32[]{:S(2)}, u32[]{:S(2)}) collective-permute-start(bf16[2,256,256]{2,1,0:T(8,128)(2,1)} %get-tuple-element.8), channel_id=1, source_target_pairs={{0,16},{1,17},{2,18},{3,19},{4,20},{5,21},{6,22},{7,23},{8,24},{9,... | collective-permute-start | bytes 786440 | tf_op jit(solution)/shard_map/ppermute | solution.py:256
  71.0 0.7 copy-start.2
  73.4 0.7 copy-start.4

commit v2 on v1

--- a/solution.py
+++ b/solution.py
@@ -11,12 +11,18 @@
 F32, BF16 = jnp.float32, jnp.bfloat16
 
 
-def call(kernel, outs, args, flops, name):
+def on_chip(array):
+    return pltpu.with_memory_space_constraint(array, pltpu.VMEM)
+
+
+def call(kernel, outs, args, flops, name, on_chip_out=()):
     moved = sum(a.size * a.dtype.itemsize for a in args)
     moved += sum(o.size * o.dtype.itemsize for o in outs)
     return pl.pallas_call(
         kernel,
-        out_shape=outs,
+        out_shape=[
+            pltpu.VMEM(o.shape, o.dtype) if i in on_chip_out else o for i, o in enumerate(outs)
+        ],
         in_specs=[VMEM] * len(args),
         out_specs=[VMEM] * len(outs),
         cost_estimate=pl.CostEstimate(flops=flops, bytes_accessed=moved, transcendentals=0),
@@ -38,7 +44,7 @@
 def pack(first, second, parts):
     _, order, columns = first.shape
     out = shaped((parts, 2, 2, order // parts, columns), first.dtype)
-    return call(pack_kernel, [out], [first, second], 0, "pack")[0]
+    return call(pack_kernel, [out], [first, second], 0, "pack", (0,))[0]
 
 
 def real_convolution(first, second, energies):
@@ -158,14 +164,14 @@
     energies, _, _, rows, columns = data.shape
     shape = (energies, 2, rows, columns)
     flops = 9 * energies * energies * rows * columns
-    return call(lesser_kernel, [shaped(shape, BF16), shaped(shape, F32)], [data], flops, "lesser")
+    return call(lesser_kernel, [shaped(shape, BF16), shaped(shape, F32)], [on_chip(data)], flops, "lesser", (0, 1))
 
 
 def retarded_convolution(lesser, retarded, exact):
     energies, _, _, rows, columns = lesser.shape
     flops = 9 * energies * energies * rows * columns
     out = shaped((energies, 2, rows, columns), BF16)
-    return call(retarded_kernel, [out], [lesser, retarded, exact], flops, "retarded")[0]
+    return call(retarded_kernel, [out], [on_chip(lesser), on_chip(retarded), on_chip(exact)], flops, "retarded", (0,))[0]
 
 
 def dot(first, second):
@@ -236,28 +242,29 @@
     left, hop = left_green.reshape(block), coupling.reshape(block)
     cube = 8 * order**3
 
-    lesser = exchange(pack(green_l, screen_l, parts))
-    retarded = exchange(pack(green_r, screen_r, parts))
+    merged = exchange(jnp.concatenate([pack(green_l, screen_l, parts), pack(green_r, screen_r, parts)], axis=1))
+    lesser, retarded = merged[:, :2], merged[:, 2:]
     sigma_lesser, exact = lesser_convolution(lesser)
     sigma_lesser = exchange(sigma_lesser)
     sigma_retarded = exchange(retarded_convolution(lesser, retarded, exact))
 
-    propagator = call(propagator_kernel, [shaped(block, BF16)], [left, hop], cube, "propagator")[0]
+    propagator = call(propagator_kernel, [shaped(block, BF16)], [left, hop], cube, "propagator", (0,))[0]
     source, state = call(
         source_kernel,
         [shaped(block, F32), shaped(block, BF16)],
-        [left, sigma_lesser],
+        [left, on_chip(sigma_lesser)],
         2 * cube,
         "source",
+        (0, 1),
     )
     devices = lax.axis_size("space")
     pairs = [(i, i + 1) for i in range(devices - 1)]
     for _ in range(devices - 1):
         entering = lax.ppermute(state, "space", pairs)
         state = call(
-            state_kernel, [shaped(block, BF16)], [source, propagator, entering], 3 * cube, "state"
+            state_kernel, [shaped(block, BF16)], [on_chip(source), on_chip(propagator), on_chip(entering)], 3 * cube, "state"
         )[0]
-    retarded_out = call(unpack_kernel, [shaped(block, BF16)], [sigma_retarded], 0, "unpack")[0]
+    retarded_out = call(unpack_kernel, [shaped(block, BF16)], [on_chip(sigma_retarded)], 0, "unpack")[0]
     return state.reshape(left_green.shape), retarded_out.reshape(left_green.shape)
 
 

time: 77.5 us -> 67.9 us (0.88)
  blocking collectives: 0 us -> 31.9 us
  waiting for transfers between devices: 33 us -> 12.3 us
  starting transfers between devices: 22.7 us -> 12 us
  Pallas kernels: 18.3 us -> 10.3 us
  local copies, waits for them, and re-layouts: 2.15 us -> 0.1 us
    all_to_all x0 -> x1, blocking collectives: none -> 31.9 us  [body(): exchange(jnp.concatenate([pack(green_l, screen_l, parts), pack(green_r, s...]
    all_to_all x2 -> x0, waiting for transfers between devices: 24 us -> none  [the longest x1 12.4 us: body(): lesser = exchange(pack(green_l, screen_l, parts))]
    all_to_all x2 -> x0, starting transfers between devices: 11.5 us -> none  [the longest x1 7.39 us: body(): lesser = exchange(pack(green_l, screen_l, parts))]
    pallas_call x8, Pallas kernels: 18.3 us -> 10.3 us  [call(): pl.pallas_call(kernel, out_shape=[pltpu.VMEM(o.shape, o.dtype) if i in on...]
    unnamed x10 -> x0, local copies, waits for them, and re-layouts: 2.15 us -> none
    all_to_all x1, waiting for transfers between devices: 1.94 us -> 3.59 us  [body(): sigma_retarded = exchange(retarded_convolution(lesser, retarded, exact))]
    all_to_all x1, waiting for transfers between devices: 7.06 us -> 8.42 us  [body(): sigma_lesser = exchange(sigma_lesser)]
    all_to_all x1, starting transfers between devices: 4.16 us -> 5.02 us  [body(): sigma_lesser = exchange(sigma_lesser)]
  transfers between devices with their start and end apart: 5 -> 3, of which waited for: 4 -> 3; matrix products, arithmetic and copies ran while one was open for 0% -> 0% of each run, Pallas kernels for 18% -> 8%
where the time goes in v2:
time: 67.9 us; the launch traced here: 67.4 us
  blocking collectives  31.9 us (47%)
  waiting for transfers between devices  12.3 us (18%)
  starting transfers between devices  12 us (18%)
  Pallas kernels  10.3 us (15%)
  between operations  0.69 us (1%)
    all_to_all x1, blocking collectives, body(): exchange(jnp.concatenate([pack(green_l, screen_l, parts), pack(green_r, s...  31.9 us
    pallas_call x8, Pallas kernels, call(): pl.pallas_call(kernel, out_shape=[pltpu.VMEM(o.shape, o.dtype) if i in on...  10.3 us
    all_to_all x1, waiting for transfers between devices, body(): sigma_lesser = exchange(sigma_lesser)  8.42 us
    all_to_all x1, starting transfers between devices, body(): sigma_lesser = exchange(sigma_lesser)  5.02 us
    all_to_all x1, waiting for transfers between devices, body(): sigma_retarded = exchange(retarded_convolution(lesser, retarded, exact))  3.59 us
    all_to_all x1, starting transfers between devices, body(): sigma_retarded = exchange(retarded_convolution(lesser, retarded, exact))  3.53 us
    ppermute x1, starting transfers between devices, body(): entering = lax.ppermute(state, 'space', pairs)  3.44 us
  transfers between devices with their start and end apart: 3, of which 3 were waited for; matrix products, arithmetic and copies ran while one was open for 0% of the time, Pallas kernels for 8%

profile of v2, /device:TPU:0, one launch (start us, length us, event | category | flops | bytes accessed | tf_op | source)
XLA Modules:
  0.0 67.4 jit_solution(13379661631240469037)
XLA Ops:
  0.6 1.1 %pack.2 = bf16[16,2,2,16,256]{4,3,2,1,0:T(8,128)(2,1)S(1)} custom-call(bf16[2,256,256]{2,1,0:T(8,128)(2,1)} %bitcast.12, bf16[2,256,256]{2,1,0:T(8,128)(2,1)} %bitcast.13), custom_call_target="tpu_custom_call" | custom-call | bytes 1048576 | tf_op jit(solution)/shard_map/pack/pallas_call | solution.py:21
  1.7 1.1 %pack.3 = bf16[16,2,2,16,256]{4,3,2,1,0:T(8,128)(2,1)S(1)} custom-call(bf16[2,256,256]{2,1,0:T(8,128)(2,1)} %bitcast.14, bf16[2,256,256]{2,1,0:T(8,128)(2,1)} %bitcast.15), custom_call_target="tpu_custom_call" | custom-call | bytes 1048576 | tf_op jit(solution)/shard_map/pack/pallas_call | solution.py:21
  2.8 0.1 pad_maximum_fusion
  2.9 31.9 %all_to_all.15 = bf16[16,4,2,16,256]{4,3,2,1,0:T(8,128)(2,1)S(1)} all-to-all(bf16[16,4,2,16,256]{4,3,2,1,0:T(8,128)(2,1)S(1)} %pad_maximum_fusion), channel_id=1, replica_groups=mesh['space'=2,'energy'=16] {'energy'}, dimensions={0} | all-to-all | bytes 2097152 | tf_op jit(solution)/shard_map/all_to_all | solution.py:245
  34.7 0.1 fusion
  34.8 1.5 %lesser.1 = (bf16[16,2,16,256]{3,2,1,0:T(8,128)(2,1)}, f32[16,2,16,256]{3,2,1,0:T(8,128)S(1)}) custom-call(bf16[16,2,2,16,256]{4,3,2,1,0:T(8,128)(2,1)S(1)} %get-tuple-element.11.data.lesser), custom_call_target="tpu_custom_call" | custom-call | flops 9437184 | bytes 1310720 | tf_op jit(solution)/shard_map/lesser/pallas_call | solution.py:21
  36.3 5.0 %all-to-all-start.1 = ((bf16[16,2,16,256]{3,2,1,0:T(8,128)(2,1)}), bf16[16,2,16,256]{3,2,1,0:T(8,128)(2,1)S(1)}, u32[]{:S(2)}, u32[]{:S(2)}) async-start(bf16[16,2,16,256]{3,2,1,0:T(8,128)(2,1)} %get-tuple-element.6), calls=%async_computation.1 | async-start | bytes 524288 | tf_op jit(solution)/shard_map/all_to_all | solution.py:248
  41.3 1.6 %retarded.1 = bf16[16,2,16,256]{3,2,1,0:T(8,128)(2,1)} custom-call(bf16[16,2,2,16,256]{4,3,2,1,0:T(8,128)(2,1)S(1)} %get-tuple-element.11.data.lesser, bf16[16,2,2,16,256]{4,3,2,1,0:T(8,128)(2,1)S(1)} %get-tuple-element.10.retarded, f32[16,2,16,256]{3,2,1,0:T(8,128)S(1)} %get-tuple-element.9.exact), custom_call_target="tpu_custom_call" | custom-call | flops 9437184 | bytes 1835008 | tf_op jit(solution)/shard_map/retarded/pallas_call | solution.py:21
  42.9 8.4 %all-to-all-done.1.sigma = bf16[16,2,16,256]{3,2,1,0:T(8,128)(2,1)S(1)} async-done(((bf16[16,2,16,256]{3,2,1,0:T(8,128)(2,1)}), bf16[16,2,16,256]{3,2,1,0:T(8,128)(2,1)S(1)}, u32[]{:S(2)}, u32[]{:S(2)}) %all-to-all-start.1) | async-done | bytes 262176 | tf_op jit(solution)/shard_map/all_to_all | solution.py:248
  51.4 3.5 %all-to-all-start.2 = ((bf16[16,2,16,256]{3,2,1,0:T(8,128)(2,1)}), bf16[16,2,16,256]{3,2,1,0:T(8,128)(2,1)S(1)}, u32[]{:S(2)}, u32[]{:S(2)}) async-start(bf16[16,2,16,256]{3,2,1,0:T(8,128)(2,1)} %retarded.1), calls=%async_computation.2 | async-start | bytes 524288 | tf_op jit(solution)/shard_map/all_to_all | solution.py:249
  54.9 1.6 %source.1 = (f32[2,256,256]{2,1,0:T(8,128)S(1)}, bf16[2,256,256]{2,1,0:T(8,128)(2,1)S(1)}) custom-call(bf16[2,256,256]{2,1,0:T(8,128)(2,1)} %bitcast.8, bf16[16,2,16,256]{3,2,1,0:T(8,128)(2,1)S(1)} %all-to-all-done.1.sigma), custom_call_target="tpu_custom_call" | custom-call | flops 268435456 | bytes 1310720 | tf_op jit(solution)/shard_map/source/pallas_call | solution.py:21
  56.5 3.4 %collective-permute-start = (bf16[2,256,256]{2,1,0:T(8,128)(2,1)S(1)}, bf16[2,256,256]{2,1,0:T(8,128)(2,1)S(1)}, u32[]{:S(2)}, u32[]{:S(2)}) collective-permute-start(bf16[2,256,256]{2,1,0:T(8,128)(2,1)S(1)} %get-tuple-element.8), channel_id=1, source_target_pairs={{0,16},{1,17},{2,18},{3,19},{4,20},{5,21},{6,22},{7,23},{8,24},{9,... | collective-permute-start | bytes 786440 | tf_op jit(solution)/shard_map/ppermute | solution.py:263
  60.0 1.3 %propagator.1 = bf16[2,256,256]{2,1,0:T(8,128)(2,1)S(1)} custom-call(bf16[2,256,256]{2,1,0:T(8,128)(2,1)} %bitcast.9, bf16[2,256,256]{2,1,0:T(8,128)(2,1)} %bitcast.10), custom_call_target="tpu_custom_call" | custom-call | flops 134217728 | bytes 786432 | tf_op jit(solution)/shard_map/propagator/pallas_call | solution.py:21
  61.3 3.6 %all-to-all-done.2.sigma = bf16[16,2,16,256]{3,2,1,0:T(8,128)(2,1)S(1)} async-done(((bf16[16,2,16,256]{3,2,1,0:T(8,128)(2,1)}), bf16[16,2,16,256]{3,2,1,0:T(8,128)(2,1)S(1)}, u32[]{:S(2)}, u32[]{:S(2)}) %all-to-all-start.2) | async-done | bytes 262176 | tf_op jit(solution)/shard_map/all_to_all | solution.py:249
  64.9 0.7 %unpack.1 = bf16[2,256,256]{2,1,0:T(8,128)(2,1)} custom-call(bf16[16,2,16,256]{3,2,1,0:T(8,128)(2,1)S(1)} %all-to-all-done.2.sigma), custom_call_target="tpu_custom_call" | custom-call | bytes 524288 | tf_op jit(solution)/shard_map/unpack/pallas_call | solution.py:21
  65.6 0.3 collective-permute-done.entering
  65.9 1.5 %state.1 = bf16[2,256,256]{2,1,0:T(8,128)(2,1)} custom-call(f32[2,256,256]{2,1,0:T(8,128)S(1)} %get-tuple-element.7.source, bf16[2,256,256]{2,1,0:T(8,128)(2,1)S(1)} %propagator.1, bf16[2,256,256]{2,1,0:T(8,128)(2,1)S(1)} %collective-permute-done.entering), custom_call_target="tpu_custom_call" | custom-call | flops 402653184 | bytes 1310720 | tf_op jit(solution)/shard_map/state/pallas_call | solution.py:21
Async XLA Ops:
  36.3 15.0 %all-to-all-start.1 = ((bf16[16,2,16,256]{3,2,1,0:T(8,128)(2,1)}), bf16[16,2,16,256]{3,2,1,0:T(8,128)(2,1)S(1)}, u32[]{:S(2)}, u32[]{:S(2)}) async-start(bf16[16,2,16,256]{3,2,1,0:T(8,128)(2,1)} %get-tuple-element.6), calls=%async_computation.1 | async-start | bytes 524288 | tf_op jit(solution)/shard_map/all_to_all | solution.py:248
  51.4 13.5 %all-to-all-start.2 = ((bf16[16,2,16,256]{3,2,1,0:T(8,128)(2,1)}), bf16[16,2,16,256]{3,2,1,0:T(8,128)(2,1)S(1)}, u32[]{:S(2)}, u32[]{:S(2)}) async-start(bf16[16,2,16,256]{3,2,1,0:T(8,128)(2,1)} %retarded.1), calls=%async_computation.2 | async-start | bytes 524288 | tf_op jit(solution)/shard_map/all_to_all | solution.py:249
  56.5 9.4 %collective-permute-start = (bf16[2,256,256]{2,1,0:T(8,128)(2,1)S(1)}, bf16[2,256,256]{2,1,0:T(8,128)(2,1)S(1)}, u32[]{:S(2)}, u32[]{:S(2)}) collective-permute-start(bf16[2,256,256]{2,1,0:T(8,128)(2,1)S(1)} %get-tuple-element.8), channel_id=1, source_target_pairs={{0,16},{1,17},{2,18},{3,19},{4,20},{5,21},{6,22},{7,23},{8,24},{9,... | collective-permute-start | bytes 786440 | tf_op jit(solution)/shard_map/ppermute | solution.py:263

commit v3 on v2

--- a/solution.py
+++ b/solution.py
@@ -15,7 +15,7 @@
     return pltpu.with_memory_space_constraint(array, pltpu.VMEM)
 
 
-def call(kernel, outs, args, flops, name, on_chip_out=()):
+def call(kernel, outs, args, flops, on_chip_out=()):
     moved = sum(a.size * a.dtype.itemsize for a in args)
     moved += sum(o.size * o.dtype.itemsize for o in outs)
     return pl.pallas_call(
@@ -26,7 +26,6 @@
         in_specs=[VMEM] * len(args),
         out_specs=[VMEM] * len(outs),
         cost_estimate=pl.CostEstimate(flops=flops, bytes_accessed=moved, transcendentals=0),
-        name=name,
     )(*args)
 
 
@@ -44,7 +43,7 @@
 def pack(first, second, parts):
     _, order, columns = first.shape
     out = shaped((parts, 2, 2, order // parts, columns), first.dtype)
-    return call(pack_kernel, [out], [first, second], 0, "pack", (0,))[0]
+    return call(pack_kernel, [out], [first, second], 0, (0,))[0]
 
 
 def real_convolution(first, second, energies):
@@ -138,7 +137,7 @@
     each_tile(rows, columns, work)
 
 
-def retarded_kernel(lesser, retarded, exact, out):
+def combine(lesser, retarded, exact, out):
     energies, _, rows, columns = out.shape
 
     def work(r, c):
@@ -164,14 +163,142 @@
     energies, _, _, rows, columns = data.shape
     shape = (energies, 2, rows, columns)
     flops = 9 * energies * energies * rows * columns
-    return call(lesser_kernel, [shaped(shape, BF16), shaped(shape, F32)], [on_chip(data)], flops, "lesser", (0, 1))
+    return call(lesser_kernel, [shaped(shape, BF16), shaped(shape, F32)], [on_chip(data)], flops, (0, 1))
 
 
 def retarded_convolution(lesser, retarded, exact):
     energies, _, _, rows, columns = lesser.shape
     flops = 9 * energies * energies * rows * columns
     out = shaped((energies, 2, rows, columns), BF16)
-    return call(retarded_kernel, [out], [on_chip(lesser), on_chip(retarded), on_chip(exact)], flops, "retarded", (0,))[0]
+    args = [on_chip(lesser), on_chip(retarded), on_chip(exact)]
+    return call(combine, [out], args, flops, (0,))[0]
+
+
+class Stages:
+    def __init__(self, parts, inner):
+        self.parts, self.inner, self.outer = parts, inner, parts // inner
+
+    def here(self):
+        me = lax.axis_index("energy")
+        return lax.div(me, self.inner), lax.rem(me, self.inner)
+
+    def place(self, me, t, s):
+        return (me[0] ^ t) * self.inner + (me[1] ^ s)
+
+    def permute(self, array, step):
+        pairs = [(i, i ^ step) for i in range(self.parts)]
+        return lax.ppermute(array, "energy", pairs)
+
+    def within(self, arrays):
+        return [self.permute(a, s) for s, a in enumerate(arrays, 1)]
+
+    def across(self, arrays):
+        sent = [self.permute(a, t * self.inner) for t, a in enumerate(arrays) if t]
+        return [arrays[0], *sent]
+
+    def call(self, kernel, outs, args, flops, scratch=(), on_chip_out=True):
+        moved = sum(a.size * a.dtype.itemsize for a in args)
+        moved += sum(o.size * o.dtype.itemsize for o in outs)
+        return pl.pallas_call(
+            functools.partial(kernel, self),
+            out_shape=[pltpu.VMEM(o.shape, o.dtype) if on_chip_out else o for o in outs],
+            in_specs=[VMEM] * len(args),
+            out_specs=[VMEM] * len(outs),
+            scratch_shapes=scratch,
+            cost_estimate=pl.CostEstimate(
+                flops=flops, bytes_accessed=moved, transcendentals=0
+            ),
+        )(*args)
+
+
+def rows_at(index, rows):
+    return pl.ds(pl.multiple_of(index * rows, rows), rows)
+
+
+def spread_kernel(stages, first, second, *outs):
+    me = stages.here()
+    rows = outs[0].shape[3]
+    for s, out in enumerate(outs, 1):
+        for o in range(stages.outer):
+            at = rows_at(o * stages.inner + (me[1] ^ s), rows)
+            for position, source in enumerate((first, second)):
+                for entry in range(2):
+                    out[o, position, entry] = source[entry, at, :]
+
+
+def gather_kernel(stages, first, second, *refs):
+    me = stages.here()
+    received, outs = refs[: stages.inner - 1], refs[stages.inner - 1 :]
+    rows = outs[0].shape[3]
+    for t, out in enumerate(outs):
+        at = rows_at(stages.place(me, t, 0), rows)
+        for position, source in enumerate((first, second)):
+            for entry in range(2):
+                out[0, position, entry] = source[entry, at, :]
+        for s, piece in enumerate(received, 1):
+            out[s] = piece[me[0] ^ t]
+
+
+def staged_in(stages, first, second):
+    _, order, columns = first.shape
+    block = (2, 2, order // stages.parts, columns)
+    pieces = []
+    if stages.inner > 1:
+        outs = [shaped((stages.outer, *block), BF16)] * (stages.inner - 1)
+        pieces = stages.call(spread_kernel, outs, [first, second], 0)
+        pieces = stages.within(pieces)
+    outs = [shaped((stages.inner, *block), BF16)] * stages.outer
+    args = [first, second, *map(on_chip, pieces)]
+    return stages.across(stages.call(gather_kernel, outs, args, 0))
+
+
+def spread_lesser_kernel(stages, *refs):
+    pieces, (data, out, exact, *spread) = refs[: stages.outer], refs[stages.outer :]
+    me = stages.here()
+    for t, piece in enumerate(pieces):
+        for s in range(stages.inner):
+            data[stages.place(me, t, s)] = piece[s]
+    lesser_kernel(data, out, exact)
+    for s, other in enumerate(spread, 1):
+        for o in range(stages.outer):
+            other[o] = out[o * stages.inner + (me[1] ^ s)]
+
+
+def regroup_kernel(stages, sigma, *refs):
+    me = stages.here()
+    received, outs = refs[: stages.inner - 1], refs[stages.inner - 1 :]
+    for t, out in enumerate(outs):
+        out[0] = sigma[stages.place(me, t, 0)]
+        for s, piece in enumerate(received, 1):
+            out[s] = piece[me[0] ^ t]
+
+
+def staged_lesser(stages, pieces):
+    _, _, _, rows, columns = pieces[0].shape
+    energies = stages.parts
+    flops = 9 * energies * energies * rows * columns
+    tile = (2, rows, columns)
+    outs = [shaped((energies, 2, *tile), BF16)]
+    outs += [shaped((energies, *tile), BF16), shaped((energies, *tile), F32)]
+    outs += [shaped((stages.outer, *tile), BF16)] * (stages.inner - 1)
+    lesser, sigma, exact, *spread = stages.call(
+        spread_lesser_kernel, outs, [on_chip(p) for p in pieces], flops
+    )
+    spread = stages.within(spread)
+    outs = [shaped((stages.inner, *tile), BF16)] * stages.outer
+    args = [on_chip(a) for a in (sigma, *spread)]
+    pieces = stages.across(stages.call(regroup_kernel, outs, args, 0))
+    return lesser, pieces, exact
+
+
+def placed(stages, pieces, out):
+    me = stages.here()
+    rows = pieces[0].shape[2]
+    for t, piece in enumerate(pieces):
+        for s in range(stages.inner):
+            at = rows_at(stages.place(me, t, s), rows)
+            for entry in range(2):
+                out[entry, at, :] = piece[s, entry]
 
 
 def dot(first, second):
@@ -190,16 +317,15 @@
     return dot_t(a, c) + dot_t(b, d), dot_t(b, c) - dot_t(a, d)
 
 
-def propagator_kernel(left, coupling, out):
-    real, imag = product(left[0], left[1], coupling[0], coupling[1])
-    out[0] = real.astype(out.dtype)
-    out[1] = imag.astype(out.dtype)
-
-
-def source_kernel(left, sigma, out, sent):
-    order = left.shape[1]
-    s_real = sigma[:, 0].reshape(order, order)
-    s_imag = sigma[:, 1].reshape(order, order)
+def propagator_real(left, coupling, out):
+    out[...] = (dot(left[0], coupling[0]) - dot(left[1], coupling[1])).astype(out.dtype)
+
+
+def propagator_imag(left, coupling, out):
+    out[...] = (dot(left[0], coupling[1]) + dot(left[1], coupling[0])).astype(out.dtype)
+
+
+def write_source(left, s_real, s_imag, out, sent):
     real, imag = product(left[0], left[1], s_real, s_imag)
     real, imag = adjoint(real.astype(BF16), imag.astype(BF16), left[0], left[1])
     out[0] = real
@@ -208,14 +334,29 @@
     sent[1] = imag.astype(sent.dtype)
 
 
+def source_kernel(left, sigma, out, sent):
+    order = left.shape[1]
+    s_real = sigma[:, 0].reshape(order, order)
+    s_imag = sigma[:, 1].reshape(order, order)
+    write_source(left, s_real, s_imag, out, sent)
+
+
+def staged_source_kernel(stages, left, *refs):
+    *pieces, out, sent, sigma = refs
+    placed(stages, pieces, sigma)
+    write_source(left, sigma[0], sigma[1], out, sent)
+
+
 def split(values):
     upper = values.astype(BF16)
     return upper, (values - upper.astype(F32)).astype(BF16)
 
 
-def state_kernel(source, propagator, entering, out):
-    p_real, p_imag = propagator[0], propagator[1]
-    real, imag = product(p_real, p_imag, entering[0], entering[1])
+def state_kernel(source, p_real, p_imag, entering, out):
+    p_real, p_imag = p_real[...], p_imag[...]
+    enters = lax.axis_index("space") > 0
+    arrived = [jnp.where(enters, entering[i], jnp.zeros_like(entering[i])) for i in range(2)]
+    real, imag = product(p_real, p_imag, *arrived)
     (real, real_low), (imag, imag_low) = split(real), split(imag)
     new_real, new_imag = adjoint(real, imag, p_real, p_imag)
     low_real, low_imag = adjoint(real_low, imag_low, p_real, p_imag)
@@ -229,42 +370,60 @@
         out[entry] = sigma[:, entry].reshape(order, order)
 
 
+INNER = 2
+
+
 def body(green_lesser, screened_lesser, green_retarded, screened_retarded, left_green, coupling):
     block = green_lesser.shape[2:]
     order = block[-1]
     assert green_lesser.shape[:2] == (1, 1) and coupling.shape[0] == 1
     parts = lax.axis_size("energy")
-    exchange = functools.partial(
-        lax.all_to_all, axis_name="energy", split_axis=0, concat_axis=0, tiled=True
-    )
+
+    def exchange(array):
+        return lax.all_to_all(array, "energy", split_axis=0, concat_axis=0, tiled=True)
+
     green_l, screen_l = green_lesser.reshape(block), screened_lesser.reshape(block)
     green_r, screen_r = green_retarded.reshape(block), screened_retarded.reshape(block)
     left, hop = left_green.reshape(block), coupling.reshape(block)
     cube = 8 * order**3
-
-    merged = exchange(jnp.concatenate([pack(green_l, screen_l, parts), pack(green_r, screen_r, parts)], axis=1))
-    lesser, retarded = merged[:, :2], merged[:, 2:]
-    sigma_lesser, exact = lesser_convolution(lesser)
-    sigma_lesser = exchange(sigma_lesser)
-    sigma_retarded = exchange(retarded_convolution(lesser, retarded, exact))
-
-    propagator = call(propagator_kernel, [shaped(block, BF16)], [left, hop], cube, "propagator", (0,))[0]
-    source, state = call(
-        source_kernel,
-        [shaped(block, F32), shaped(block, BF16)],
-        [left, on_chip(sigma_lesser)],
-        2 * cube,
-        "source",
-        (0, 1),
-    )
+    staged = parts & (parts - 1) == 0 and order // parts % 8 == 0
+
+    if staged:
+        stages = Stages(parts, INNER)
+        pieces = staged_in(stages, green_l, screen_l)
+        lesser, sigma_lesser, exact = staged_lesser(stages, pieces)
+    else:
+        lesser = exchange(pack(green_l, screen_l, parts))
+        sigma_lesser, exact = lesser_convolution(lesser)
+        sigma_lesser = exchange(sigma_lesser)
+    packed = pack(green_r, screen_r, parts)
+    retarded = exchange(packed)
+    sigma_retarded = retarded_convolution(lesser, retarded, exact)
+    args = [on_chip(exchange(sigma_retarded))]
+    retarded_out = call(unpack_kernel, [shaped(block, BF16)], args, 0)[0]
+
+    propagator = []
+    for kernel in (propagator_real, propagator_imag):
+        out = [shaped(block[1:], BF16)]
+        propagator += call(kernel, out, [left, hop], cube // 2, (0,))
+    outs = [shaped(block, F32), shaped(block, BF16)]
+    if staged:
+        args = [left, *map(on_chip, sigma_lesser)]
+        scratch = [pltpu.VMEM(block, BF16)]
+        source, state = stages.call(staged_source_kernel, outs, args, 2 * cube, scratch)
+    else:
+        args = [left, on_chip(sigma_lesser)]
+        source, state = call(source_kernel, outs, args, 2 * cube, (0, 1))
     devices = lax.axis_size("space")
-    pairs = [(i, i + 1) for i in range(devices - 1)]
+    pairs = [(i, (i + 1) % devices) for i in range(devices)]
     for _ in range(devices - 1):
         entering = lax.ppermute(state, "space", pairs)
         state = call(
-            state_kernel, [shaped(block, BF16)], [on_chip(source), on_chip(propagator), on_chip(entering)], 3 * cube, "state"
+            state_kernel,
+            [shaped(block, BF16)],
+            [on_chip(a) for a in (source, *propagator, entering)],
+            3 * cube,
         )[0]
-    retarded_out = call(unpack_kernel, [shaped(block, BF16)], [on_chip(sigma_retarded)], 0, "unpack")[0]
     return state.reshape(left_green.shape), retarded_out.reshape(left_green.shape)
 
 

time: 67.9 us -> 70.4 us (1.037)
  blocking collectives: 31.9 us -> 0 us
  starting transfers between devices: 12 us -> 37.1 us
  waiting for transfers between devices: 12.3 us -> 19.4 us
  Pallas kernels: 10.3 us -> 12.8 us
    all_to_all x1 -> x0, blocking collectives: 31.9 us -> none  [body(): exchange(jnp.concatenate([pack(green_l, screen_l, parts), pack(green_r, s...]
    ppermute x0 -> x16, starting transfers between devices: none -> 23.8 us  [permute(): return lax.ppermute(array, 'energy', pairs)]
    ppermute x0 -> x16, waiting for transfers between devices: none -> 17 us  [permute(): return lax.ppermute(array, 'energy', pairs)]
    all_to_all x2, waiting for transfers between devices: 12 us -> 0.01 us  [exchange(): lax.all_to_all(array, 'energy', split_axis=0, concat_axis=0, tiled=True)]
    pallas_call x0 -> x5, Pallas kernels: none -> 4.58 us  [call(): pl.pallas_call(functools.partial(kernel, self), out_shape=[pltpu.VMEM(o.s...]
    all_to_all x2, starting transfers between devices: 8.56 us -> 11.7 us  [exchange(): lax.all_to_all(array, 'energy', split_axis=0, concat_axis=0, tiled=True)]
    pallas_call x8 -> x6, Pallas kernels: 10.3 us -> 8.19 us  [call(): pl.pallas_call(kernel, out_shape=[pltpu.VMEM(o.shape, o.dtype) if i in on...]
    ppermute x1, waiting for transfers between devices: 0.33 us -> 2.33 us  [body(): entering = lax.ppermute(state, 'space', pairs)]
  transfers between devices with their start and end apart: 3 -> 19, of which waited for: 3 -> 7; matrix products, arithmetic and copies ran while one was open for 0% -> 0% of each run, Pallas kernels for 8% -> 15%
where the time goes in v3:
time: 70.4 us; the launch traced here: 69.9 us
  starting transfers between devices  37.1 us (53%)
  waiting for transfers between devices  19.4 us (28%)
  Pallas kernels  12.8 us (18%)
  between operations  0.73 us (1%)
    ppermute x16, starting transfers between devices, permute(): return lax.ppermute(array, 'energy', pairs)  23.8 us
    ppermute x16, waiting for transfers between devices, permute(): return lax.ppermute(array, 'energy', pairs)  17 us
    all_to_all x2, starting transfers between devices, exchange(): lax.all_to_all(array, 'energy', split_axis=0, concat_axis=0, tiled=True)  11.7 us
    pallas_call x6, Pallas kernels, call(): pl.pallas_call(kernel, out_shape=[pltpu.VMEM(o.shape, o.dtype) if i in on...  8.19 us
    pallas_call x5, Pallas kernels, call(): pl.pallas_call(functools.partial(kernel, self), out_shape=[pltpu.VMEM(o.s...  4.58 us
    ppermute x1, waiting for transfers between devices, body(): entering = lax.ppermute(state, 'space', pairs)  2.33 us
    ppermute x1, starting transfers between devices, body(): entering = lax.ppermute(state, 'space', pairs)  1.58 us
  transfers between devices with their start and end apart: 19, of which 7 were waited for; matrix products, arithmetic and copies ran while one was open for 0% of the time, Pallas kernels for 15%

profile of v3, /device:TPU:0, one launch (start us, length us, event | category | flops | bytes accessed | tf_op | source)
XLA Modules:
  0.0 69.9 jit_solution(11362109189936796302)
XLA Ops:
  0.6 1.9 %shard_map.85 = bf16[16,2,2,16,256]{4,3,2,1,0:T(8,128)(2,1)} custom-call(bf16[2,256,256]{2,1,0:T(8,128)(2,1)} %bitcast.18, bf16[2,256,256]{2,1,0:T(8,128)(2,1)} %bitcast.19), custom_call_target="tpu_custom_call" | custom-call | bytes 1048576 | tf_op jit(solution)/shard_map/pallas_call | solution.py:21
  2.5 7.4 %all-to-all-start = ((bf16[16,2,2,16,256]{4,3,2,1,0:T(8,128)(2,1)}), bf16[16,2,2,16,256]{4,3,2,1,0:T(8,128)(2,1)S(1)}, u32[]{:S(2)}, u32[]{:S(2)}) async-start(bf16[16,2,2,16,256]{4,3,2,1,0:T(8,128)(2,1)} %shard_map.85), calls=%async_computation | async-start | bytes 1048576 | tf_op jit(solution)/shard_map/all_to_all | solution.py:383
  9.9 1.1 %shard_map.77 = bf16[8,2,2,16,256]{4,3,2,1,0:T(8,128)(2,1)S(1)} custom-call(bf16[2,256,256]{2,1,0:T(8,128)(2,1)} %bitcast.8, bf16[2,256,256]{2,1,0:T(8,128)(2,1)} %bitcast.10), custom_call_target="tpu_custom_call" | custom-call | bytes 786432 | tf_op jit(solution)/shard_map/pallas_call | solution.py:202
  10.9 0.5 collective-permute-start
  11.4 1.2 %collective-permute-done.refs_0_ = bf16[8,2,2,16,256]{4,3,2,1,0:T(8,128)(2,1)S(1)} collective-permute-done((bf16[8,2,2,16,256]{4,3,2,1,0:T(8,128)(2,1)S(1)}, bf16[8,2,2,16,256]{4,3,2,1,0:T(8,128)(2,1)S(1)}, u32[]{:S(2)}, u32[]{:S(2)}) %collective-permute-start) | collective-permute-done | bytes 262176 | tf_op jit(solution)/shard_map/ppermute | solution.py:190
  12.6 1.1 %shard_map.78 = (bf16[2,2,2,16,256]{4,3,2,1,0:T(8,128)(2,1)S(1)}, bf16[2,2,2,16,256]{4,3,2,1,0:T(8,128)(2,1)S(1)}, bf16[2,2,2,16,256]{4,3,2,1,0:T(8,128)(2,1)S(1...) custom-call(bf16[2,256,256]{2,1,0:T(8,128)(2,1)} %bitcast.9, ...), custom_call_target="tpu_custom_call" | custom-call | bytes 1310720 | tf_op jit(solution)/shard_map/pallas_call | solution.py:202
  13.7 2.0 %collective-permute-start.1 = (bf16[2,2,2,16,256]{4,3,2,1,0:T(8,128)(2,1)S(1)}, bf16[2,2,2,16,256]{4,3,2,1,0:T(8,128)(2,1)S(1)}, u32[]{:S(2)}, u32[]{:S(2)}) collective-permute-start(bf16[2,2,2,16,256]{4,3,2,1,0:T(8,128)(2,1)S(1)} %get-tuple-element.25), channel_id=1, source_target_pairs={{0,2},{1,3},{2,0},{3,1},{4,6},{5,7},{6,4},{7,5},{8,10},{9,11},{10,... | collective-permute-start | bytes 196616 | tf_op jit(solution)/shard_map/ppermute | solution.py:190
  15.6 1.5 %collective-permute-start.2 = (bf16[2,2,2,16,256]{4,3,2,1,0:T(8,128)(2,1)S(1)}, bf16[2,2,2,16,256]{4,3,2,1,0:T(8,128)(2,1)S(1)}, u32[]{:S(2)}, u32[]{:S(2)}) collective-permute-start(bf16[2,2,2,16,256]{4,3,2,1,0:T(8,128)(2,1)S(1)} %get-tuple-element.26), channel_id=1, source_target_pairs={{0,4},{1,5},{2,6},{3,7},{4,0},{5,1},{6,2},{7,3},{8,12},{9,13},{10,... | collective-permute-start | bytes 196616 | tf_op jit(solution)/shard_map/ppermute | solution.py:190
  17.1 0.1 collective-permute-start.3
  17.2 2.8 %collective-permute-start.4 = (bf16[2,2,2,16,256]{4,3,2,1,0:T(8,128)(2,1)S(1)}, bf16[2,2,2,16,256]{4,3,2,1,0:T(8,128)(2,1)S(1)}, u32[]{:S(2)}, u32[]{:S(2)}) collective-permute-start(bf16[2,2,2,16,256]{4,3,2,1,0:T(8,128)(2,1)S(1)} %get-tuple-element.28), channel_id=1, source_target_pairs={{0,8},{1,9},{2,10},{3,11},{4,12},{5,13},{6,14},{7,15},{8,0},{9,1},... | collective-permute-start | bytes 196616 | tf_op jit(solution)/shard_map/ppermute | solution.py:190
  20.0 1.5 %collective-permute-start.5 = (bf16[2,2,2,16,256]{4,3,2,1,0:T(8,128)(2,1)S(1)}, bf16[2,2,2,16,256]{4,3,2,1,0:T(8,128)(2,1)S(1)}, u32[]{:S(2)}, u32[]{:S(2)}) collective-permute-start(bf16[2,2,2,16,256]{4,3,2,1,0:T(8,128)(2,1)S(1)} %get-tuple-element.29), channel_id=1, source_target_pairs={{0,10},{1,11},{2,8},{3,9},{4,14},{5,15},{6,12},{7,13},{8,2},{9,3},... | collective-permute-start | bytes 196616 | tf_op jit(solution)/shard_map/ppermute | solution.py:190
  21.5 0.0 collective-permute-done.1.refs_1_
  21.5 3.3 %collective-permute-start.6 = (bf16[2,2,2,16,256]{4,3,2,1,0:T(8,128)(2,1)S(1)}, bf16[2,2,2,16,256]{4,3,2,1,0:T(8,128)(2,1)S(1)}, u32[]{:S(2)}, u32[]{:S(2)}) collective-permute-start(bf16[2,2,2,16,256]{4,3,2,1,0:T(8,128)(2,1)S(1)} %get-tuple-element.30), channel_id=1, source_target_pairs={{0,12},{1,13},{2,14},{3,15},{4,8},{5,9},{6,10},{7,11},{8,4},{9,5},... | collective-permute-start | bytes 196616 | tf_op jit(solution)/shard_map/ppermute | solution.py:190
  24.7 0.0 collective-permute-done.2.refs_2_
  24.7 1.0 %collective-permute-start.7 = (bf16[2,2,2,16,256]{4,3,2,1,0:T(8,128)(2,1)S(1)}, bf16[2,2,2,16,256]{4,3,2,1,0:T(8,128)(2,1)S(1)}, u32[]{:S(2)}, u32[]{:S(2)}) collective-permute-start(bf16[2,2,2,16,256]{4,3,2,1,0:T(8,128)(2,1)S(1)} %get-tuple-element.31), channel_id=1, source_target_pairs={{0,14},{1,15},{2,12},{3,13},{4,10},{5,11},{6,8},{7,9},{8,6},{9,7},... | collective-permute-start | bytes 196616 | tf_op jit(solution)/shard_map/ppermute | solution.py:190
  25.7 0.0 collective-permute-done.3.refs_3_
  25.7 7.0 %collective-permute-done.4.refs_4_ = bf16[2,2,2,16,256]{4,3,2,1,0:T(8,128)(2,1)S(1)} collective-permute-done((bf16[2,2,2,16,256]{4,3,2,1,0:T(8,128)(2,1)S(1)}, bf16[2,2,2,16,256]{4,3,2,1,0:T(8,128)(2,1)S(1)}, u32[]{:S(2)}, u32[]{:S(2)}) %collective-permute-start.4) | collective-permute-done | bytes 65568 | tf_op jit(solution)/shard_map/ppermute | solution.py:190
  32.7 2.3 %collective-permute-done.5.refs_5_ = bf16[2,2,2,16,256]{4,3,2,1,0:T(8,128)(2,1)S(1)} collective-permute-done((bf16[2,2,2,16,256]{4,3,2,1,0:T(8,128)(2,1)S(1)}, bf16[2,2,2,16,256]{4,3,2,1,0:T(8,128)(2,1)S(1)}, u32[]{:S(2)}, u32[]{:S(2)}) %collective-permute-start.5) | collective-permute-done | bytes 65568 | tf_op jit(solution)/shard_map/ppermute | solution.py:190
  35.0 0.0 collective-permute-done.6.refs_6_
  35.0 0.0 collective-permute-done.7.refs_7_
  35.0 0.8 %shard_map.79 = (bf16[16,2,2,16,256]{4,3,2,1,0:T(8,128)(2,1)S(1)}, bf16[16,2,16,256]{3,2,1,0:T(8,128)(2,1)S(1)}, f32[16,2,16,256]{3,2,1,0:T(8,128)S(1)}, bf16[8,2,16,256]{3,2,1,0:T(8,128)(2,1)S(1)}) custom-call(bf16[2,2,2,16,256]{4,3,2,1,0:T(8,128)(2,1)S(1)} %get-tuple-element.24.refs_0_, bf16[2,2,2,16,256]{4,3,2,1,0:T(8,128)(2,1)S(1)} %collective-permute-done.1.refs_1_, ...), custom_call_target="tpu_custom_call" | custom-call | flops 9437184 | bytes 1966080 | tf_op jit(solution)/shard_map/pallas_call | solution.py:202
  35.8 0.1 collective-permute-start.8
  35.9 0.0 all-to-all-done.retarded
  35.9 1.6 %shard_map.86 = bf16[16,2,16,256]{3,2,1,0:T(8,128)(2,1)} custom-call(bf16[16,2,2,16,256]{4,3,2,1,0:T(8,128)(2,1)S(1)} %get-tuple-element.44.lesser, bf16[16,2,2,16,256]{4,3,2,1,0:T(8,128)(2,1)S(1)} %all-to-all-done.retarded, f32[16,2,16,256]{3,2,1,0:T(8,128)S(1)} %get-tuple-element.45.exact), custom_call_target="tpu_custom_call" | custom-call | flops 9437184 | bytes 1835008 | tf_op jit(solution)/shard_map/pallas_call | solution.py:21
  37.5 4.3 %all-to-all-start.1 = ((bf16[16,2,16,256]{3,2,1,0:T(8,128)(2,1)}), bf16[16,2,16,256]{3,2,1,0:T(8,128)(2,1)S(1)}, u32[]{:S(2)}, u32[]{:S(2)}) async-start(bf16[16,2,16,256]{3,2,1,0:T(8,128)(2,1)} %shard_map.86), calls=%async_computation.1 | async-start | bytes 524288 | tf_op jit(solution)/shard_map/all_to_all | solution.py:383
  41.9 0.0 collective-permute-done.8.refs_0_
  41.9 2.0 %collective-permute-start.9 = (bf16[2,2,16,256]{3,2,1,0:T(8,128)(2,1)S(1)}, bf16[2,2,16,256]{3,2,1,0:T(8,128)(2,1)S(1)}, u32[]{:S(2)}, u32[]{:S(2)}) collective-permute-start(bf16[2,2,16,256]{3,2,1,0:T(8,128)(2,1)S(1)} %get-tuple-element.35), channel_id=1, source_target_pairs={{0,2},{1,3},{2,0},{3,1},{4,6},{5,7},{6,4},{7,5},{8,10},{9,11},{10,... | collective-permute-start | bytes 98312 | tf_op jit(solution)/shard_map/ppermute | solution.py:190
  43.9 1.5 %collective-permute-start.10 = (bf16[2,2,16,256]{3,2,1,0:T(8,128)(2,1)S(1)}, bf16[2,2,16,256]{3,2,1,0:T(8,128)(2,1)S(1)}, u32[]{:S(2)}, u32[]{:S(2)}) collective-permute-start(bf16[2,2,16,256]{3,2,1,0:T(8,128)(2,1)S(1)} %get-tuple-element.36), channel_id=1, source_target_pairs={{0,4},{1,5},{2,6},{3,7},{4,0},{5,1},{6,2},{7,3},{8,12},{9,13},{10,... | collective-permute-start | bytes 98312 | tf_op jit(solution)/shard_map/ppermute | solution.py:190
  45.4 0.1 collective-permute-start.11
  45.5 2.8 %collective-permute-start.12 = (bf16[2,2,16,256]{3,2,1,0:T(8,128)(2,1)S(1)}, bf16[2,2,16,256]{3,2,1,0:T(8,128)(2,1)S(1)}, u32[]{:S(2)}, u32[]{:S(2)}) collective-permute-start(bf16[2,2,16,256]{3,2,1,0:T(8,128)(2,1)S(1)} %get-tuple-element.38), channel_id=1, source_target_pairs={{0,8},{1,9},{2,10},{3,11},{4,12},{5,13},{6,14},{7,15},{8,0},{9,1},... | collective-permute-start | bytes 98312 | tf_op jit(solution)/shard_map/ppermute | solution.py:190
  48.3 1.5 %collective-permute-start.13 = (bf16[2,2,16,256]{3,2,1,0:T(8,128)(2,1)S(1)}, bf16[2,2,16,256]{3,2,1,0:T(8,128)(2,1)S(1)}, u32[]{:S(2)}, u32[]{:S(2)}) collective-permute-start(bf16[2,2,16,256]{3,2,1,0:T(8,128)(2,1)S(1)} %get-tuple-element.39), channel_id=1, source_target_pairs={{0,10},{1,11},{2,8},{3,9},{4,14},{5,15},{6,12},{7,13},{8,2},{9,3},... | collective-permute-start | bytes 98312 | tf_op jit(solution)/shard_map/ppermute | solution.py:190
  49.8 0.0 collective-permute-done.9.refs_1_
  49.8 3.3 %collective-permute-start.14 = (bf16[2,2,16,256]{3,2,1,0:T(8,128)(2,1)S(1)}, bf16[2,2,16,256]{3,2,1,0:T(8,128)(2,1)S(1)}, u32[]{:S(2)}, u32[]{:S(2)}) collective-permute-start(bf16[2,2,16,256]{3,2,1,0:T(8,128)(2,1)S(1)} %get-tuple-element.40), channel_id=1, source_target_pairs={{0,12},{1,13},{2,14},{3,15},{4,8},{5,9},{6,10},{7,11},{8,4},{9,5},... | collective-permute-start | bytes 98312 | tf_op jit(solution)/shard_map/ppermute | solution.py:190
  53.0 0.0 collective-permute-done.10.refs_2_
  53.0 0.1 collective-permute-start.15
  53.1 0.0 collective-permute-done.11.refs_3_
  53.1 0.9 %collective-permute-done.12.refs_4_ = bf16[2,2,16,256]{3,2,1,0:T(8,128)(2,1)S(1)} collective-permute-done((bf16[2,2,16,256]{3,2,1,0:T(8,128)(2,1)S(1)}, bf16[2,2,16,256]{3,2,1,0:T(8,128)(2,1)S(1)}, u32[]{:S(2)}, u32[]{:S(2)}) %collective-permute-start.12) | collective-permute-done | bytes 32800 | tf_op jit(solution)/shard_map/ppermute | solution.py:190
  54.1 2.4 %collective-permute-done.13.refs_5_ = bf16[2,2,16,256]{3,2,1,0:T(8,128)(2,1)S(1)} collective-permute-done((bf16[2,2,16,256]{3,2,1,0:T(8,128)(2,1)S(1)}, bf16[2,2,16,256]{3,2,1,0:T(8,128)(2,1)S(1)}, u32[]{:S(2)}, u32[]{:S(2)}) %collective-permute-start.13) | collective-permute-done | bytes 32800 | tf_op jit(solution)/shard_map/ppermute | solution.py:190
  56.5 0.0 collective-permute-done.14.refs_6_
  56.5 3.2 %collective-permute-done.15.refs_7_ = bf16[2,2,16,256]{3,2,1,0:T(8,128)(2,1)S(1)} collective-permute-done((bf16[2,2,16,256]{3,2,1,0:T(8,128)(2,1)S(1)}, bf16[2,2,16,256]{3,2,1,0:T(8,128)(2,1)S(1)}, u32[]{:S(2)}, u32[]{:S(2)}) %collective-permute-start.15) | collective-permute-done | bytes 32800 | tf_op jit(solution)/shard_map/ppermute | solution.py:190
  59.6 1.6 %shard_map.81 = (f32[2,256,256]{2,1,0:T(8,128)S(1)}, bf16[2,256,256]{2,1,0:T(8,128)(2,1)S(1)}) custom-call(bf16[2,256,256]{2,1,0:T(8,128)(2,1)} %bitcast.12, bf16[2,2,16,256]{3,2,1,0:T(8,128)(2,1)S(1)} %get-tuple-element.34.refs_0_, bf16[2,2,16,256]{3,2,1,0:T(8,128)(2,1)S(1)} %collective-permute-done.9.refs_1_, ...), custom_call_target="tpu_custom_call" | custom-call | flops 268435456 | bytes 1310720 | tf_op jit(solution)/shard_map/pallas_call | solution.py:202
  61.3 1.6 %collective-permute-start.16 = (bf16[2,256,256]{2,1,0:T(8,128)(2,1)S(1)}, bf16[2,256,256]{2,1,0:T(8,128)(2,1)S(1)}, u32[]{:S(2)}, u32[]{:S(2)}) collective-permute-start(bf16[2,256,256]{2,1,0:T(8,128)(2,1)S(1)} %get-tuple-element.43), channel_id=1, source_target_pairs={{0,16},{16,0},{1,17},{17,1},{2,18},{18,2},{3,19},{19,3},{4,20},{20... | collective-permute-start | bytes 786440 | tf_op jit(solution)/shard_map/ppermute | solution.py:420
  62.9 1.3 %shard_map.82.p_real = bf16[256,256]{1,0:T(8,128)(2,1)S(1)} custom-call(bf16[2,256,256]{2,1,0:T(8,128)(2,1)} %bitcast.13, bf16[2,256,256]{2,1,0:T(8,128)(2,1)} %bitcast.15), custom_call_target="tpu_custom_call" | custom-call | flops 67108864 | bytes 655360 | tf_op jit(solution)/shard_map/pallas_call | solution.py:21
  64.1 1.3 %shard_map.83.p_imag = bf16[256,256]{1,0:T(8,128)(2,1)S(1)} custom-call(bf16[2,256,256]{2,1,0:T(8,128)(2,1)} %bitcast.14, bf16[2,256,256]{2,1,0:T(8,128)(2,1)} %bitcast.16), custom_call_target="tpu_custom_call" | custom-call | flops 67108864 | bytes 655360 | tf_op jit(solution)/shard_map/pallas_call | solution.py:21
  65.4 2.3 %collective-permute-done.16.entering = bf16[2,256,256]{2,1,0:T(8,128)(2,1)S(1)} collective-permute-done((bf16[2,256,256]{2,1,0:T(8,128)(2,1)S(1)}, bf16[2,256,256]{2,1,0:T(8,128)(2,1)S(1)}, u32[]{:S(2)}, u32[]{:S(2)}) %collective-permute-start.16) | collective-permute-done | bytes 262176 | tf_op jit(solution)/shard_map/ppermute | solution.py:420
  67.7 1.5 %shard_map.84 = bf16[2,256,256]{2,1,0:T(8,128)(2,1)} custom-call(f32[2,256,256]{2,1,0:T(8,128)S(1)} %get-tuple-element.42.source, bf16[256,256]{1,0:T(8,128)(2,1)S(1)} %shard_map.82.p_real, bf16[256,256]{1,0:T(8,128)(2,1)S(1)} %shard_map.83.p_imag, bf16[2,256,256]{2,1,0:T(8,128)(2,1)S(1)} %collective-permute-done.16.entering), custom_call_target="tpu_custom_call" | custom-call | flops 402653184 | bytes 1310720 | tf_op jit(solution)/shard_map/pallas_call | solution.py:21
  69.2 0.0 all-to-all-done.1.sigma
  69.2 0.7 %shard_map.87 = bf16[2,256,256]{2,1,0:T(8,128)(2,1)} custom-call(bf16[16,2,16,256]{3,2,1,0:T(8,128)(2,1)S(1)} %all-to-all-done.1.sigma), custom_call_target="tpu_custom_call" | custom-call | bytes 524288 | tf_op jit(solution)/shard_map/pallas_call | solution.py:21
  (1 shorter events, 0.0 us)
Async XLA Ops:
  2.5 33.4 %all-to-all-start = ((bf16[16,2,2,16,256]{4,3,2,1,0:T(8,128)(2,1)}), bf16[16,2,2,16,256]{4,3,2,1,0:T(8,128)(2,1)S(1)}, u32[]{:S(2)}, u32[]{:S(2)}) async-start(bf16[16,2,2,16,256]{4,3,2,1,0:T(8,128)(2,1)} %shard_map.85), calls=%async_computation | async-start | bytes 1048576 | tf_op jit(solution)/shard_map/all_to_all | solution.py:383
  10.9 1.6 %collective-permute-start = (bf16[8,2,2,16,256]{4,3,2,1,0:T(8,128)(2,1)S(1)}, bf16[8,2,2,16,256]{4,3,2,1,0:T(8,128)(2,1)S(1)}, u32[]{:S(2)}, u32[]{:S(2)}) collective-permute-start(bf16[8,2,2,16,256]{4,3,2,1,0:T(8,128)(2,1)S(1)} %shard_map.77), channel_id=1, source_target_pairs={{0,1},{1,0},{2,3},{3,2},{4,5},{5,4},{6,7},{7,6},{8,9},{9,8},{10,11... | collective-permute-start | bytes 786440 | tf_op jit(solution)/shard_map/ppermute | solution.py:190
  13.7 7.8 %collective-permute-start.1 = (bf16[2,2,2,16,256]{4,3,2,1,0:T(8,128)(2,1)S(1)}, bf16[2,2,2,16,256]{4,3,2,1,0:T(8,128)(2,1)S(1)}, u32[]{:S(2)}, u32[]{:S(2)}) collective-permute-start(bf16[2,2,2,16,256]{4,3,2,1,0:T(8,128)(2,1)S(1)} %get-tuple-element.25), channel_id=1, source_target_pairs={{0,2},{1,3},{2,0},{3,1},{4,6},{5,7},{6,4},{7,5},{8,10},{9,11},{10,... | collective-permute-start | bytes 196616 | tf_op jit(solution)/shard_map/ppermute | solution.py:190
  15.6 9.1 %collective-permute-start.2 = (bf16[2,2,2,16,256]{4,3,2,1,0:T(8,128)(2,1)S(1)}, bf16[2,2,2,16,256]{4,3,2,1,0:T(8,128)(2,1)S(1)}, u32[]{:S(2)}, u32[]{:S(2)}) collective-permute-start(bf16[2,2,2,16,256]{4,3,2,1,0:T(8,128)(2,1)S(1)} %get-tuple-element.26), channel_id=1, source_target_pairs={{0,4},{1,5},{2,6},{3,7},{4,0},{5,1},{6,2},{7,3},{8,12},{9,13},{10,... | collective-permute-start | bytes 196616 | tf_op jit(solution)/shard_map/ppermute | solution.py:190
  17.1 8.6 %collective-permute-start.3 = (bf16[2,2,2,16,256]{4,3,2,1,0:T(8,128)(2,1)S(1)}, bf16[2,2,2,16,256]{4,3,2,1,0:T(8,128)(2,1)S(1)}, u32[]{:S(2)}, u32[]{:S(2)}) collective-permute-start(bf16[2,2,2,16,256]{4,3,2,1,0:T(8,128)(2,1)S(1)} %get-tuple-element.27), channel_id=1, source_target_pairs={{0,6},{1,7},{2,4},{3,5},{4,2},{5,3},{6,0},{7,1},{8,14},{9,15},{10,... | collective-permute-start | bytes 196616 | tf_op jit(solution)/shard_map/ppermute | solution.py:190
  17.2 15.5 %collective-permute-start.4 = (bf16[2,2,2,16,256]{4,3,2,1,0:T(8,128)(2,1)S(1)}, bf16[2,2,2,16,256]{4,3,2,1,0:T(8,128)(2,1)S(1)}, u32[]{:S(2)}, u32[]{:S(2)}) collective-permute-start(bf16[2,2,2,16,256]{4,3,2,1,0:T(8,128)(2,1)S(1)} %get-tuple-element.28), channel_id=1, source_target_pairs={{0,8},{1,9},{2,10},{3,11},{4,12},{5,13},{6,14},{7,15},{8,0},{9,1},... | collective-permute-start | bytes 196616 | tf_op jit(solution)/shard_map/ppermute | solution.py:190
  20.0 15.0 %collective-permute-start.5 = (bf16[2,2,2,16,256]{4,3,2,1,0:T(8,128)(2,1)S(1)}, bf16[2,2,2,16,256]{4,3,2,1,0:T(8,128)(2,1)S(1)}, u32[]{:S(2)}, u32[]{:S(2)}) collective-permute-start(bf16[2,2,2,16,256]{4,3,2,1,0:T(8,128)(2,1)S(1)} %get-tuple-element.29), channel_id=1, source_target_pairs={{0,10},{1,11},{2,8},{3,9},{4,14},{5,15},{6,12},{7,13},{8,2},{9,3},... | collective-permute-start | bytes 196616 | tf_op jit(solution)/shard_map/ppermute | solution.py:190
  21.5 13.6 %collective-permute-start.6 = (bf16[2,2,2,16,256]{4,3,2,1,0:T(8,128)(2,1)S(1)}, bf16[2,2,2,16,256]{4,3,2,1,0:T(8,128)(2,1)S(1)}, u32[]{:S(2)}, u32[]{:S(2)}) collective-permute-start(bf16[2,2,2,16,256]{4,3,2,1,0:T(8,128)(2,1)S(1)} %get-tuple-element.30), channel_id=1, source_target_pairs={{0,12},{1,13},{2,14},{3,15},{4,8},{5,9},{6,10},{7,11},{8,4},{9,5},... | collective-permute-start | bytes 196616 | tf_op jit(solution)/shard_map/ppermute | solution.py:190
  24.7 10.3 %collective-permute-start.7 = (bf16[2,2,2,16,256]{4,3,2,1,0:T(8,128)(2,1)S(1)}, bf16[2,2,2,16,256]{4,3,2,1,0:T(8,128)(2,1)S(1)}, u32[]{:S(2)}, u32[]{:S(2)}) collective-permute-start(bf16[2,2,2,16,256]{4,3,2,1,0:T(8,128)(2,1)S(1)} %get-tuple-element.31), channel_id=1, source_target_pairs={{0,14},{1,15},{2,12},{3,13},{4,10},{5,11},{6,8},{7,9},{8,6},{9,7},... | collective-permute-start | bytes 196616 | tf_op jit(solution)/shard_map/ppermute | solution.py:190
  35.8 6.0 %collective-permute-start.8 = (bf16[8,2,16,256]{3,2,1,0:T(8,128)(2,1)S(1)}, bf16[8,2,16,256]{3,2,1,0:T(8,128)(2,1)S(1)}, u32[]{:S(2)}, u32[]{:S(2)}) collective-permute-start(bf16[8,2,16,256]{3,2,1,0:T(8,128)(2,1)S(1)} %get-tuple-element.33), channel_id=1, source_target_pairs={{0,1},{1,0},{2,3},{3,2},{4,5},{5,4},{6,7},{7,6},{8,9},{9,8},{10,11... | collective-permute-start | bytes 393224 | tf_op jit(solution)/shard_map/ppermute | solution.py:190
  37.5 31.7 %all-to-all-start.1 = ((bf16[16,2,16,256]{3,2,1,0:T(8,128)(2,1)}), bf16[16,2,16,256]{3,2,1,0:T(8,128)(2,1)S(1)}, u32[]{:S(2)}, u32[]{:S(2)}) async-start(bf16[16,2,16,256]{3,2,1,0:T(8,128)(2,1)} %shard_map.86), calls=%async_computation.1 | async-start | bytes 524288 | tf_op jit(solution)/shard_map/all_to_all | solution.py:383
  41.9 7.8 %collective-permute-start.9 = (bf16[2,2,16,256]{3,2,1,0:T(8,128)(2,1)S(1)}, bf16[2,2,16,256]{3,2,1,0:T(8,128)(2,1)S(1)}, u32[]{:S(2)}, u32[]{:S(2)}) collective-permute-start(bf16[2,2,16,256]{3,2,1,0:T(8,128)(2,1)S(1)} %get-tuple-element.35), channel_id=1, source_target_pairs={{0,2},{1,3},{2,0},{3,1},{4,6},{5,7},{6,4},{7,5},{8,10},{9,11},{10,... | collective-permute-start | bytes 98312 | tf_op jit(solution)/shard_map/ppermute | solution.py:190
  43.9 9.1 %collective-permute-start.10 = (bf16[2,2,16,256]{3,2,1,0:T(8,128)(2,1)S(1)}, bf16[2,2,16,256]{3,2,1,0:T(8,128)(2,1)S(1)}, u32[]{:S(2)}, u32[]{:S(2)}) collective-permute-start(bf16[2,2,16,256]{3,2,1,0:T(8,128)(2,1)S(1)} %get-tuple-element.36), channel_id=1, source_target_pairs={{0,4},{1,5},{2,6},{3,7},{4,0},{5,1},{6,2},{7,3},{8,12},{9,13},{10,... | collective-permute-start | bytes 98312 | tf_op jit(solution)/shard_map/ppermute | solution.py:190
  45.4 7.8 %collective-permute-start.11 = (bf16[2,2,16,256]{3,2,1,0:T(8,128)(2,1)S(1)}, bf16[2,2,16,256]{3,2,1,0:T(8,128)(2,1)S(1)}, u32[]{:S(2)}, u32[]{:S(2)}) collective-permute-start(bf16[2,2,16,256]{3,2,1,0:T(8,128)(2,1)S(1)} %get-tuple-element.37), channel_id=1, source_target_pairs={{0,6},{1,7},{2,4},{3,5},{4,2},{5,3},{6,0},{7,1},{8,14},{9,15},{10,... | collective-permute-start | bytes 98312 | tf_op jit(solution)/shard_map/ppermute | solution.py:190
  45.5 8.6 %collective-permute-start.12 = (bf16[2,2,16,256]{3,2,1,0:T(8,128)(2,1)S(1)}, bf16[2,2,16,256]{3,2,1,0:T(8,128)(2,1)S(1)}, u32[]{:S(2)}, u32[]{:S(2)}) collective-permute-start(bf16[2,2,16,256]{3,2,1,0:T(8,128)(2,1)S(1)} %get-tuple-element.38), channel_id=1, source_target_pairs={{0,8},{1,9},{2,10},{3,11},{4,12},{5,13},{6,14},{7,15},{8,0},{9,1},... | collective-permute-start | bytes 98312 | tf_op jit(solution)/shard_map/ppermute | solution.py:190
  48.3 8.2 %collective-permute-start.13 = (bf16[2,2,16,256]{3,2,1,0:T(8,128)(2,1)S(1)}, bf16[2,2,16,256]{3,2,1,0:T(8,128)(2,1)S(1)}, u32[]{:S(2)}, u32[]{:S(2)}) collective-permute-start(bf16[2,2,16,256]{3,2,1,0:T(8,128)(2,1)S(1)} %get-tuple-element.39), channel_id=1, source_target_pairs={{0,10},{1,11},{2,8},{3,9},{4,14},{5,15},{6,12},{7,13},{8,2},{9,3},... | collective-permute-start | bytes 98312 | tf_op jit(solution)/shard_map/ppermute | solution.py:190
  49.8 6.7 %collective-permute-start.14 = (bf16[2,2,16,256]{3,2,1,0:T(8,128)(2,1)S(1)}, bf16[2,2,16,256]{3,2,1,0:T(8,128)(2,1)S(1)}, u32[]{:S(2)}, u32[]{:S(2)}) collective-permute-start(bf16[2,2,16,256]{3,2,1,0:T(8,128)(2,1)S(1)} %get-tuple-element.40), channel_id=1, source_target_pairs={{0,12},{1,13},{2,14},{3,15},{4,8},{5,9},{6,10},{7,11},{8,4},{9,5},... | collective-permute-start | bytes 98312 | tf_op jit(solution)/shard_map/ppermute | solution.py:190
  53.0 6.6 %collective-permute-start.15 = (bf16[2,2,16,256]{3,2,1,0:T(8,128)(2,1)S(1)}, bf16[2,2,16,256]{3,2,1,0:T(8,128)(2,1)S(1)}, u32[]{:S(2)}, u32[]{:S(2)}) collective-permute-start(bf16[2,2,16,256]{3,2,1,0:T(8,128)(2,1)S(1)} %get-tuple-element.41), channel_id=1, source_target_pairs={{0,14},{1,15},{2,12},{3,13},{4,10},{5,11},{6,8},{7,9},{8,6},{9,7},... | collective-permute-start | bytes 98312 | tf_op jit(solution)/shard_map/ppermute | solution.py:190
  61.3 6.4 %collective-permute-start.16 = (bf16[2,256,256]{2,1,0:T(8,128)(2,1)S(1)}, bf16[2,256,256]{2,1,0:T(8,128)(2,1)S(1)}, u32[]{:S(2)}, u32[]{:S(2)}) collective-permute-start(bf16[2,256,256]{2,1,0:T(8,128)(2,1)S(1)} %get-tuple-element.43), channel_id=1, source_target_pairs={{0,16},{16,0},{1,17},{17,1},{2,18},{18,2},{3,19},{19,3},{4,20},{20... | collective-permute-start | bytes 786440 | tf_op jit(solution)/shard_map/ppermute | solution.py:420
